TPU v7x, 512 devices: a whole 4x4x16 slice. The times are simulated.
512 devices in a mesh: img: 32 (over z, y_hi), comp: 2 (over y_lo), ref: 8 (over x, core).
Axes of the slice: x: 4, y: 4 (y_hi: 2, y_lo: 2; y = y_hi * 2 + y_lo), z: 16, core: 2. Of those that a mesh axis runs over, the one named last changes fastest.
Arguments:
- images: float32 [3072, 16384], P('img', 'comp'), may hold values from -24 to 24
- references: float32 [2048, 16384], P(('img', 'ref'), 'comp'), may hold values from -0.140625 to 0.140625
Outputs:
- weighted_sums: float32 [2048, 16384], P(('img', 'ref'), 'comp')
All inputs are finite; a program needn't handle non-finite values.
Results may differ from a plain program's by a relative error of at most 0.0003.
Values sent between devices are 32-bit elements; how exact they have to be, the bound alone decides.
No kernel may reach another device: no remote copies, remote signals or barrier semaphores. Data moves between devices by JAX's collectives and lax.ppermute only.
A program may use at most 64 MiB of HBM per device.

v0:
```python
import functools

import jax
import jax.numpy as jnp
from jax import lax
from jax.experimental import pallas as pl
from jax.experimental.pallas import tpu as pltpu
from jax.sharding import Mesh, PartitionSpec as P


HIGHEST = lax.Precision.HIGHEST
PLANE = ("core", "yl", "x")
OWNERS = ("yh", "x", "core")


def moved(value, axis, steps):
    count = lax.axis_size(axis)
    return lax.ppermute(value, axis, [(i, (i + steps) % count) for i in range(count)])


def both(value, axis):
    other = moved(value, axis, 1)
    first = lax.axis_index(axis) == 0
    return jnp.stack([jnp.where(first, value, other), jnp.where(first, other, value)])


def cut_kernel(at_ref, images_ref, out_ref, sem):
    width = out_ref.shape[1]
    columns = pl.ds(pl.multiple_of(at_ref[0] * width, width), width)
    copy = pltpu.make_async_copy(images_ref.at[:, columns], out_ref, sem)
    copy.start()
    copy.wait()


def cut(images, which, width):
    return pl.pallas_call(
        cut_kernel,
        out_shape=jax.ShapeDtypeStruct((images.shape[0], width), jnp.float32),
        in_specs=[pl.BlockSpec(memory_space=pltpu.SMEM),
                  pl.BlockSpec(memory_space=pltpu.HBM)],
        out_specs=pl.BlockSpec(memory_space=pltpu.VMEM),
        scratch_shapes=[pltpu.SemaphoreType.DMA(())],
        name="cut",
    )(which.reshape(1).astype(jnp.int32), images)


def weighted_kernel(starts, at_ref, post_ref, *refs):
    count = len(starts)
    blocks, (out_ref, held, order, sems) = refs[:count], refs[count:]
    copies = []
    for k, block in enumerate(blocks):
        copies.append(pltpu.make_async_copy(
            block, held.at[pl.ds(starts[k], block.shape[0])], sems.at[k]))
        copies[-1].start()
    for k, block in enumerate(blocks):
        size = block.shape[0]
        row = pl.multiple_of(at_ref[k], 8)
        order[starts[k]:starts[k] + size, :] = post_ref[pl.ds(row, size), :]
    tile = 256
    pieces = 3
    part = held.shape[0] // pieces
    waited = 0
    for piece in range(pieces):
        stop = (piece + 1) * part
        while waited < count and starts[waited] < stop:
            copies[waited].wait()
            waited += 1
        rows = pl.ds(piece * part, part)
        post = order[rows, :].T

        @pl.loop(0, out_ref.shape[1] // tile)
        def _(t):
            columns = pl.ds(pl.multiple_of(t * tile, tile), tile)
            term = jnp.dot(post, held[rows, columns], precision=HIGHEST,
                           preferred_element_type=jnp.float32)
            if piece == 0:
                out_ref[:, columns] = term
            else:
                out_ref[:, columns] += term


def weighted(at, post, blocks):
    images, refs = post.shape
    width = blocks[0].shape[1]
    starts = [0]
    for block in blocks[:-1]:
        starts.append(starts[-1] + block.shape[0])
    return pl.pallas_call(
        functools.partial(weighted_kernel, starts),
        out_shape=jax.ShapeDtypeStruct((refs, width), jnp.float32),
        in_specs=[pl.BlockSpec(memory_space=pltpu.SMEM),
                  pl.BlockSpec(memory_space=pltpu.VMEM)]
        + [pl.BlockSpec(memory_space=pl.ANY)] * len(blocks),
        out_specs=pl.BlockSpec(memory_space=pltpu.VMEM),
        scratch_shapes=[pltpu.VMEM((images, width), jnp.float32),
                        pltpu.VMEM((images, refs), jnp.float32),
                        pltpu.SemaphoreType.DMA((len(blocks),))],
        cost_estimate=pl.CostEstimate(
            flops=12 * images * refs * width, bytes_accessed=8 * images * width,
            transcendentals=0),
        name="weighted",
    )(at, post, *blocks)


def step_on_shards(images, references):
    count_z = lax.axis_size("z")
    slices = lax.axis_size("x") * lax.axis_size("core")
    width = images.shape[1] // slices
    here = lax.axis_index("z")
    own = cut(images, lax.axis_index(("x", "core")), width)
    rows = own.shape[0]

    pieces = references.reshape(references.shape[0], slices, width).transpose(1, 0, 2)
    half = lax.all_to_all(pieces, ("x", "core"), 0, 0, tiled=True)
    plane_refs = both(half, "yh").reshape(-1, width)
    halfnorm = 0.5 * jnp.sum(plane_refs * plane_refs, axis=1)

    partial = jnp.zeros((count_z * rows, plane_refs.shape[0]), jnp.float32)
    blocks, offsets, firsts = [], [], []

    def place(partial, block, offset, first_row):
        scores = lax.dot_general(
            block, plane_refs, (((1,), (1,)), ((), ())),
            precision=HIGHEST, preferred_element_type=jnp.float32) - halfnorm[None, :]
        blocks.append(block)
        offsets.append(offset)
        firsts.append(first_row)
        row = (here + offset) % count_z * rows + first_row
        return lax.dynamic_update_slice_in_dim(partial, scores, row, 0)

    partial = place(partial, own, 0, 0)
    right = left = own
    for step in range(1, count_z // 2 + 1):
        middle = 0
        if step == count_z // 2:
            middle = rows // 2
            right, left = right[:middle], left[middle:]
        right = moved(right, "z", 1)
        left = moved(left, "z", -1)
        partial = place(partial, right, -step, 0)
        partial = place(partial, left, step, middle)

    partial = partial.reshape(count_z, rows, -1)
    scores = jnp.sum(lax.all_to_all(partial, PLANE, 0, 0, tiled=False), axis=0)

    largest = jnp.max(scores, axis=1)
    expon = jnp.exp(scores - largest[:, None])
    totals = jnp.sum(expon, axis=1)
    stats = jnp.stack([largest, totals])
    everyone = lax.all_to_all(
        jnp.broadcast_to(stats[None], (count_z,) + stats.shape), "z", 0, 0, tiled=False)
    top = jnp.max(everyone[:, 0], axis=0)
    total = jnp.sum(everyone[:, 1] * jnp.exp(everyone[:, 0] - top), axis=0)
    post = expon * (jnp.exp(largest - top) / total)[:, None]
    chips = lax.axis_size("yl") * lax.axis_size("x")
    spread = lax.all_to_all(
        jnp.broadcast_to(post[None], (chips,) + post.shape), ("yl", "x"), 0, 0, tiled=False)
    post = lax.all_gather(spread, "core").reshape(-1, post.shape[1])

    at = (here + jnp.array(offsets, jnp.int32)) % count_z * rows + jnp.array(firsts, jnp.int32)
    out = weighted(at, post, blocks)

    owners = lax.axis_size("yh") * slices
    back = lax.all_to_all(out.reshape(owners, -1, width), OWNERS, 0, 0, tiled=False)
    mine_rows = jnp.sum(back.reshape(lax.axis_size("yh"), slices, -1, width), axis=0)
    return mine_rows.transpose(1, 0, 2).reshape(references.shape)


def solution(mesh):
    fine = Mesh(mesh.devices.reshape(16, 2, 2, 4, 2), ("z", "yh", "yl", "x", "core"))
    return jax.shard_map(
        step_on_shards,
        mesh=fine,
        in_specs=(P(("z", "yh"), "yl"), P(("z", "yh", "x", "core"), "yl")),
        out_specs=P(("z", "yh", "x", "core"), "yl"),
        check_vma=False,
    )
```

profile of v0, /device:TPU:6, one launch (start us, length us, event | category | flops | bytes accessed | tf_op | source)
XLA Modules:
  0.0 191.1 jit_solution(2730805923310829462)
XLA Ops:
  0.0 9.2 %all-to-all-start = ((f32[8,8,1024]{2,1,0:T(8,128)}), f32[8,8,1024]{2,1,0:T(8,128)S(1)}, u32[]{:S(2)}, u32[]{:S(2)}) async-start(f32[8,8,1024]{2,1,0:T(8,128)} %bitcast.77), calls=%async_computation | async-start | bytes 524288 | tf_op jit(solution)/shard_map/all_to_all | solution.py:114
  13.0 7.0 %collective-permute-start.2 = (f32[96,1024]{1,0:T(8,128)}, f32[96,1024]{1,0:T(8,128)S(1)}, u32[]{:S(2)}, u32[]{:S(2)}) collective-permute-start(f32[96,1024]{1,0:T(8,128)} %cut.1.refs_0_), channel_id=1, source_target_pairs={{0,480},{32,0},{64,32},{96,64},{128,96},{160,128},{192,160},{224,1... | collective-permute-start | bytes 1179656 | tf_op jit(solution)/shard_map/ppermute | solution.py:18
  20.0 5.1 %collective-permute-start = (f32[8,8,1024]{2,1,0:T(8,128)S(1)}, f32[8,8,1024]{2,1,0:T(8,128)S(1)}, u32[]{:S(2)}, u32[]{:S(2)}) collective-permute-start(f32[8,8,1024]{2,1,0:T(8,128)S(1)} %all-to-all-done), channel_id=1, source_target_pairs={{0,16},{16,0},{1,17},{17,1},{2,18},{18,2},{3,19},{19,3},{4,20},{20... | collective-permute-start | bytes 786440 | tf_op jit(solution)/shard_map/ppermute | solution.py:18
  25.5 2.2 %collective-permute-done.1.refs_1_ = f32[96,1024]{1,0:T(8,128)S(1)} collective-permute-done((f32[96,1024]{1,0:T(8,128)}, f32[96,1024]{1,0:T(8,128)S(1)}, u32[]{:S(2)}, u32[]{:S(2)}) %collective-permute-start.1) | collective-permute-done | bytes 393248 | tf_op jit(solution)/shard_map/ppermute | solution.py:18
  29.6 5.1 %collective-permute-start.4 = (f32[96,1024]{1,0:T(8,128)S(1)}, f32[96,1024]{1,0:T(8,128)S(1)}, u32[]{:S(2)}, u32[]{:S(2)}) collective-permute-start(f32[96,1024]{1,0:T(8,128)S(1)} %collective-permute-done.2.refs_2_), channel_id=1, source_target_pairs={{0,480},{32,0},{64,32},{96,64},{128,96},{160,128},{192,160},{224,1... | collective-permute-start | bytes 1179656 | tf_op jit(solution)/shard_map/ppermute | solution.py:18
  37.0 4.3 %collective-permute-done.3.refs_3_ = f32[96,1024]{1,0:T(8,128)S(1)} collective-permute-done((f32[96,1024]{1,0:T(8,128)S(1)}, f32[96,1024]{1,0:T(8,128)S(1)}, u32[]{:S(2)}, u32[]{:S(2)}) %collective-permute-start.3) | collective-permute-done | bytes 393248 | tf_op jit(solution)/shard_map/ppermute | solution.py:18
  43.3 5.1 %collective-permute-start.6 = (f32[96,1024]{1,0:T(8,128)S(1)}, f32[96,1024]{1,0:T(8,128)S(1)}, u32[]{:S(2)}, u32[]{:S(2)}) collective-permute-start(f32[96,1024]{1,0:T(8,128)S(1)} %collective-permute-done.4.refs_4_), channel_id=1, source_target_pairs={{0,480},{32,0},{64,32},{96,64},{128,96},{160,128},{192,160},{224,1... | collective-permute-start | bytes 1179656 | tf_op jit(solution)/shard_map/ppermute | solution.py:18
  49.7 4.4 %collective-permute-done.5.refs_5_ = f32[96,1024]{1,0:T(8,128)S(1)} collective-permute-done((f32[96,1024]{1,0:T(8,128)S(1)}, f32[96,1024]{1,0:T(8,128)S(1)}, u32[]{:S(2)}, u32[]{:S(2)}) %collective-permute-start.5) | collective-permute-done | bytes 393248 | tf_op jit(solution)/shard_map/ppermute | solution.py:18
  56.1 5.1 %collective-permute-start.8 = (f32[96,1024]{1,0:T(8,128)S(1)}, f32[96,1024]{1,0:T(8,128)S(1)}, u32[]{:S(2)}, u32[]{:S(2)}) collective-permute-start(f32[96,1024]{1,0:T(8,128)S(1)} %collective-permute-done.6.refs_6_), channel_id=1, source_target_pairs={{0,480},{32,0},{64,32},{96,64},{128,96},{160,128},{192,160},{224,1... | collective-permute-start | bytes 1179656 | tf_op jit(solution)/shard_map/ppermute | solution.py:18
  62.5 3.6 %collective-permute-done.7.refs_7_ = f32[96,1024]{1,0:T(8,128)S(1)} collective-permute-done((f32[96,1024]{1,0:T(8,128)S(1)}, f32[96,1024]{1,0:T(8,128)S(1)}, u32[]{:S(2)}, u32[]{:S(2)}) %collective-permute-start.7) | collective-permute-done | bytes 393248 | tf_op jit(solution)/shard_map/ppermute | solution.py:18
  68.0 5.1 %collective-permute-start.10 = (f32[96,1024]{1,0:T(8,128)S(1)}, f32[96,1024]{1,0:T(8,128)S(1)}, u32[]{:S(2)}, u32[]{:S(2)}) collective-permute-start(f32[96,1024]{1,0:T(8,128)S(1)} %collective-permute-done.8.refs_8_), channel_id=1, source_target_pairs={{0,480},{32,0},{64,32},{96,64},{128,96},{160,128},{192,160},{224,1... | collective-permute-start | bytes 1179656 | tf_op jit(solution)/shard_map/ppermute | solution.py:18
  74.4 2.7 %collective-permute-done.9.refs_9_ = f32[96,1024]{1,0:T(8,128)S(1)} collective-permute-done((f32[96,1024]{1,0:T(8,128)S(1)}, f32[96,1024]{1,0:T(8,128)S(1)}, u32[]{:S(2)}, u32[]{:S(2)}) %collective-permute-start.9) | collective-permute-done | bytes 393248 | tf_op jit(solution)/shard_map/ppermute | solution.py:18
  79.1 5.1 %collective-permute-start.12 = (f32[96,1024]{1,0:T(8,128)S(1)}, f32[96,1024]{1,0:T(8,128)S(1)}, u32[]{:S(2)}, u32[]{:S(2)}) collective-permute-start(f32[96,1024]{1,0:T(8,128)S(1)} %collective-permute-done.10.refs_10_), channel_id=1, source_target_pairs={{0,480},{32,0},{64,32},{96,64},{128,96},{160,128},{192,160},{224,1... | collective-permute-start | bytes 1179656 | tf_op jit(solution)/shard_map/ppermute | solution.py:18
  85.6 2.5 %collective-permute-done.11.refs_11_ = f32[96,1024]{1,0:T(8,128)S(1)} collective-permute-done((f32[96,1024]{1,0:T(8,128)S(1)}, f32[96,1024]{1,0:T(8,128)S(1)}, u32[]{:S(2)}, u32[]{:S(2)}) %collective-permute-start.11) | collective-permute-done | bytes 393248 | tf_op jit(solution)/shard_map/ppermute | solution.py:18
  90.0 5.1 %collective-permute-start.14 = (f32[96,1024]{1,0:T(8,128)S(1)}, f32[96,1024]{1,0:T(8,128)S(1)}, u32[]{:S(2)}, u32[]{:S(2)}) collective-permute-start(f32[96,1024]{1,0:T(8,128)S(1)} %collective-permute-done.12.refs_12_), channel_id=1, source_target_pairs={{0,480},{32,0},{64,32},{96,64},{128,96},{160,128},{192,160},{224,1... | collective-permute-start | bytes 1179656 | tf_op jit(solution)/shard_map/ppermute | solution.py:18
  96.4 3.0 %collective-permute-done.13.refs_13_ = f32[96,1024]{1,0:T(8,128)S(1)} collective-permute-done((f32[96,1024]{1,0:T(8,128)S(1)}, f32[96,1024]{1,0:T(8,128)S(1)}, u32[]{:S(2)}, u32[]{:S(2)}) %collective-permute-start.13) | collective-permute-done | bytes 393248 | tf_op jit(solution)/shard_map/ppermute | solution.py:18
  101.4 5.4 %collective-permute-start.16 = (f32[48,1024]{1,0:T(8,128)S(1)}, f32[48,1024]{1,0:T(8,128)S(1)}, u32[]{:S(2)}, u32[]{:S(2)}) collective-permute-start(f32[48,1024]{1,0:T(8,128)S(1)} %slice.18), channel_id=1, source_target_pairs={{0,480},{32,0},{64,32},{96,64},{128,96},{160,128},{192,160},{224,1... | collective-permute-start | bytes 589832 | tf_op jit(solution)/shard_map/ppermute | solution.py:18
  110.6 16.8 %all_to_all.25 = f32[16,96,128]{2,1,0:T(8,128)S(1)} all-to-all(f32[16,96,128]{2,1,0:T(8,128)S(1)} %bitcast.73), channel_id=1, replica_groups=mesh['z'=16,'yh'=2,'yl'=2,'x'=4,'core'=2] {'core','yl','x'}, dimensions={0} | all-to-all | bytes 1572864 | tf_op jit(solution)/shard_map/all_to_all | solution.py:144
  127.8 21.7 %all_to_all.26 = f32[16,2,96]{2,1,0:T(2,128)S(1)} all-to-all(f32[16,2,96]{2,1,0:T(2,128)S(1)} %broadcast_in_dim.7), channel_id=1, replica_groups=mesh['z'=16,'yh'=2,'yl'=2,'x'=4,'core'=2] {'z'}, dimensions={0} | all-to-all | bytes 24576 | tf_op jit(solution)/shard_map/all_to_all | solution.py:150
  150.5 5.6 %all-to-all-start.3 = ((f32[8,96,128]{2,1,0:T(8,128)}), f32[8,96,128]{2,1,0:T(8,128)S(1)}, u32[]{:S(2)}, u32[]{:S(2)}) async-start(f32[8,96,128]{2,1,0:T(8,128)} %broadcast_in_dim.8), calls=%async_computation.3 | async-start | bytes 786432 | tf_op jit(solution)/shard_map/all_to_all | solution.py:156
  156.8 5.3 %all-to-all-done.3 = f32[8,96,128]{2,1,0:T(8,128)S(1)} async-done(((f32[8,96,128]{2,1,0:T(8,128)}), f32[8,96,128]{2,1,0:T(8,128)S(1)}, u32[]{:S(2)}, u32[]{:S(2)}) %all-to-all-start.3) | async-done | bytes 393248 | tf_op jit(solution)/shard_map/all_to_all | solution.py:156
  162.0 2.5 %all-gather = f32[16,96,128]{2,1,0:T(8,128)} all-gather(f32[8,96,128]{2,1,0:T(8,128)S(1)} %all-to-all-done.3), channel_id=2, replica_groups=mesh['z'=16,'yh'=2,'yl'=2,'x'=4,'core'=2] {'core'}, dimensions={0}, use_global_device_ids=true | all-gather | bytes 1179648 | tf_op jit(solution)/shard_map/all_gather | solution.py:158
  164.5 9.5 %weighted.1 = f32[128,1024]{1,0:T(8,128)} custom-call(s32[17]{0:T(128)} %fusion.21.at_ref, f32[1536,128]{1,0:T(8,128)} %bitcast.75, f32[96,1024]{1,0:T(8,128)} %cut.1.refs_0_, f32[96,1024]{1,0:T(8,128)} %copy-done.3, f32[96,1024]{1,0:T(8,128)} %copy-done.4, f32[96,1024]{1,0:T(8,128)} %copy-done.5, f32[96,1024]{1,0:T(8,128)} %copy-done.6, ...), custom_call_target="tpu_custom_call" | custom-call | flops 2415919104 | bytes 12582912 | tf_op jit(solution)/shard_map/weighted/pallas_call | solution.py:88
  174.0 16.3 %all_to_all.27 = f32[16,8,1024]{2,1,0:T(8,128)S(1)} all-to-all(f32[16,8,1024]{2,1,0:T(8,128)} %bitcast.76), channel_id=1, replica_groups=mesh['z'=16,'yh'=2,'yl'=2,'x'=4,'core'=2] {'yh','x','core'}, dimensions={0} | all-to-all | bytes 1048576 | tf_op jit(solution)/shard_map/all_to_all | solution.py:164
  (95 shorter events, 32.3 us)
Async XLA Ops:
  0.0 20.0 %all-to-all-start = ((f32[8,8,1024]{2,1,0:T(8,128)}), f32[8,8,1024]{2,1,0:T(8,128)S(1)}, u32[]{:S(2)}, u32[]{:S(2)}) async-start(f32[8,8,1024]{2,1,0:T(8,128)} %bitcast.77), calls=%async_computation | async-start | bytes 524288 | tf_op jit(solution)/shard_map/all_to_all | solution.py:114
  11.0 16.7 %collective-permute-start.1 = (f32[96,1024]{1,0:T(8,128)}, f32[96,1024]{1,0:T(8,128)S(1)}, u32[]{:S(2)}, u32[]{:S(2)}) collective-permute-start(f32[96,1024]{1,0:T(8,128)} %cut.1.refs_0_), channel_id=1, source_target_pairs={{0,32},{32,64},{64,96},{96,128},{128,160},{160,192},{192,224},{224... | collective-permute-start | bytes 1179656 | tf_op jit(solution)/shard_map/ppermute | solution.py:18
  13.0 16.6 %collective-permute-start.2 = (f32[96,1024]{1,0:T(8,128)}, f32[96,1024]{1,0:T(8,128)S(1)}, u32[]{:S(2)}, u32[]{:S(2)}) collective-permute-start(f32[96,1024]{1,0:T(8,128)} %cut.1.refs_0_), channel_id=1, source_target_pairs={{0,480},{32,0},{64,32},{96,64},{128,96},{160,128},{192,160},{224,1... | collective-permute-start | bytes 1179656 | tf_op jit(solution)/shard_map/ppermute | solution.py:18
  20.0 14.7 %collective-permute-start = (f32[8,8,1024]{2,1,0:T(8,128)S(1)}, f32[8,8,1024]{2,1,0:T(8,128)S(1)}, u32[]{:S(2)}, u32[]{:S(2)}) collective-permute-start(f32[8,8,1024]{2,1,0:T(8,128)S(1)} %all-to-all-done), channel_id=1, source_target_pairs={{0,16},{16,0},{1,17},{17,1},{2,18},{18,2},{3,19},{19,3},{4,20},{20... | collective-permute-start | bytes 786440 | tf_op jit(solution)/shard_map/ppermute | solution.py:18
  27.7 13.7 %collective-permute-start.3 = (f32[96,1024]{1,0:T(8,128)S(1)}, f32[96,1024]{1,0:T(8,128)S(1)}, u32[]{:S(2)}, u32[]{:S(2)}) collective-permute-start(f32[96,1024]{1,0:T(8,128)S(1)} %collective-permute-done.1.refs_1_), channel_id=1, source_target_pairs={{0,32},{32,64},{64,96},{96,128},{128,160},{160,192},{192,224},{224... | collective-permute-start | bytes 1179656 | tf_op jit(solution)/shard_map/ppermute | solution.py:18
  29.6 13.6 %collective-permute-start.4 = (f32[96,1024]{1,0:T(8,128)S(1)}, f32[96,1024]{1,0:T(8,128)S(1)}, u32[]{:S(2)}, u32[]{:S(2)}) collective-permute-start(f32[96,1024]{1,0:T(8,128)S(1)} %collective-permute-done.2.refs_2_), channel_id=1, source_target_pairs={{0,480},{32,0},{64,32},{96,64},{128,96},{160,128},{192,160},{224,1... | collective-permute-start | bytes 1179656 | tf_op jit(solution)/shard_map/ppermute | solution.py:18
  41.3 43.5 %copy-start.5 = (f32[96,1024]{1,0:T(8,128)}, f32[96,1024]{1,0:T(8,128)S(1)}, u32[]{:S(2)}) copy-start(f32[96,1024]{1,0:T(8,128)S(1)} %collective-permute-done.3.refs_3_) | copy-start | bytes 1179652
  41.4 12.8 %collective-permute-start.5 = (f32[96,1024]{1,0:T(8,128)S(1)}, f32[96,1024]{1,0:T(8,128)S(1)}, u32[]{:S(2)}, u32[]{:S(2)}) collective-permute-start(f32[96,1024]{1,0:T(8,128)S(1)} %collective-permute-done.3.refs_3_), channel_id=1, source_target_pairs={{0,32},{32,64},{64,96},{96,128},{128,160},{160,192},{192,224},{224... | collective-permute-start | bytes 1179656 | tf_op jit(solution)/shard_map/ppermute | solution.py:18
  43.3 12.8 %collective-permute-start.6 = (f32[96,1024]{1,0:T(8,128)S(1)}, f32[96,1024]{1,0:T(8,128)S(1)}, u32[]{:S(2)}, u32[]{:S(2)}) collective-permute-start(f32[96,1024]{1,0:T(8,128)S(1)} %collective-permute-done.4.refs_4_), channel_id=1, source_target_pairs={{0,480},{32,0},{64,32},{96,64},{128,96},{160,128},{192,160},{224,1... | collective-permute-start | bytes 1179656 | tf_op jit(solution)/shard_map/ppermute | solution.py:18
  54.1 11.9 %collective-permute-start.7 = (f32[96,1024]{1,0:T(8,128)S(1)}, f32[96,1024]{1,0:T(8,128)S(1)}, u32[]{:S(2)}, u32[]{:S(2)}) collective-permute-start(f32[96,1024]{1,0:T(8,128)S(1)} %collective-permute-done.5.refs_5_), channel_id=1, source_target_pairs={{0,32},{32,64},{64,96},{96,128},{128,160},{160,192},{192,224},{224... | collective-permute-start | bytes 1179656 | tf_op jit(solution)/shard_map/ppermute | solution.py:18
  56.1 11.9 %collective-permute-start.8 = (f32[96,1024]{1,0:T(8,128)S(1)}, f32[96,1024]{1,0:T(8,128)S(1)}, u32[]{:S(2)}, u32[]{:S(2)}) collective-permute-start(f32[96,1024]{1,0:T(8,128)S(1)} %collective-permute-done.6.refs_6_), channel_id=1, source_target_pairs={{0,480},{32,0},{64,32},{96,64},{128,96},{160,128},{192,160},{224,1... | collective-permute-start | bytes 1179656 | tf_op jit(solution)/shard_map/ppermute | solution.py:18
  66.1 11.1 %collective-permute-start.9 = (f32[96,1024]{1,0:T(8,128)S(1)}, f32[96,1024]{1,0:T(8,128)S(1)}, u32[]{:S(2)}, u32[]{:S(2)}) collective-permute-start(f32[96,1024]{1,0:T(8,128)S(1)} %collective-permute-done.7.refs_7_), channel_id=1, source_target_pairs={{0,32},{32,64},{64,96},{96,128},{128,160},{160,192},{192,224},{224... | collective-permute-start | bytes 1179656 | tf_op jit(solution)/shard_map/ppermute | solution.py:18
  68.0 11.1 %collective-permute-start.10 = (f32[96,1024]{1,0:T(8,128)S(1)}, f32[96,1024]{1,0:T(8,128)S(1)}, u32[]{:S(2)}, u32[]{:S(2)}) collective-permute-start(f32[96,1024]{1,0:T(8,128)S(1)} %collective-permute-done.8.refs_8_), channel_id=1, source_target_pairs={{0,480},{32,0},{64,32},{96,64},{128,96},{160,128},{192,160},{224,1... | collective-permute-start | bytes 1179656 | tf_op jit(solution)/shard_map/ppermute | solution.py:18
  77.2 10.9 %collective-permute-start.11 = (f32[96,1024]{1,0:T(8,128)S(1)}, f32[96,1024]{1,0:T(8,128)S(1)}, u32[]{:S(2)}, u32[]{:S(2)}) collective-permute-start(f32[96,1024]{1,0:T(8,128)S(1)} %collective-permute-done.9.refs_9_), channel_id=1, source_target_pairs={{0,32},{32,64},{64,96},{96,128},{128,160},{160,192},{192,224},{224... | collective-permute-start | bytes 1179656 | tf_op jit(solution)/shard_map/ppermute | solution.py:18
  79.1 10.9 %collective-permute-start.12 = (f32[96,1024]{1,0:T(8,128)S(1)}, f32[96,1024]{1,0:T(8,128)S(1)}, u32[]{:S(2)}, u32[]{:S(2)}) collective-permute-start(f32[96,1024]{1,0:T(8,128)S(1)} %collective-permute-done.10.refs_10_), channel_id=1, source_target_pairs={{0,480},{32,0},{64,32},{96,64},{128,96},{160,128},{192,160},{224,1... | collective-permute-start | bytes 1179656 | tf_op jit(solution)/shard_map/ppermute | solution.py:18
  88.0 11.3 %collective-permute-start.13 = (f32[96,1024]{1,0:T(8,128)S(1)}, f32[96,1024]{1,0:T(8,128)S(1)}, u32[]{:S(2)}, u32[]{:S(2)}) collective-permute-start(f32[96,1024]{1,0:T(8,128)S(1)} %collective-permute-done.11.refs_11_), channel_id=1, source_target_pairs={{0,32},{32,64},{64,96},{96,128},{128,160},{160,192},{192,224},{224... | collective-permute-start | bytes 1179656 | tf_op jit(solution)/shard_map/ppermute | solution.py:18
  90.0 11.3 %collective-permute-start.14 = (f32[96,1024]{1,0:T(8,128)S(1)}, f32[96,1024]{1,0:T(8,128)S(1)}, u32[]{:S(2)}, u32[]{:S(2)}) collective-permute-start(f32[96,1024]{1,0:T(8,128)S(1)} %collective-permute-done.12.refs_12_), channel_id=1, source_target_pairs={{0,480},{32,0},{64,32},{96,64},{128,96},{160,128},{192,160},{224,1... | collective-permute-start | bytes 1179656 | tf_op jit(solution)/shard_map/ppermute | solution.py:18
  99.4 8.8 %collective-permute-start.15 = (f32[48,1024]{1,0:T(8,128)S(1)}, f32[48,1024]{1,0:T(8,128)S(1)}, u32[]{:S(2)}, u32[]{:S(2)}) collective-permute-start(f32[48,1024]{1,0:T(8,128)S(1)} %slice.17), channel_id=1, source_target_pairs={{0,32},{32,64},{64,96},{96,128},{128,160},{160,192},{192,224},{224... | collective-permute-start | bytes 589832 | tf_op jit(solution)/shard_map/ppermute | solution.py:18
  101.4 8.5 %collective-permute-start.16 = (f32[48,1024]{1,0:T(8,128)S(1)}, f32[48,1024]{1,0:T(8,128)S(1)}, u32[]{:S(2)}, u32[]{:S(2)}) collective-permute-start(f32[48,1024]{1,0:T(8,128)S(1)} %slice.18), channel_id=1, source_target_pairs={{0,480},{32,0},{64,32},{96,64},{128,96},{160,128},{192,160},{224,1... | collective-permute-start | bytes 589832 | tf_op jit(solution)/shard_map/ppermute | solution.py:18
  107.4 48.8 %copy-start.17 = (s32[17]{0:T(128)S(1)}, s32[17]{0:T(128)}, u32[]{:S(2)}) copy-start(s32[17]{0:T(128)} %constant.155.clone) | copy-start | bytes 208
  107.4 48.8 %copy-start.18 = (s32[17]{0:T(128)S(1)}, s32[17]{0:T(128)}, u32[]{:S(2)}) copy-start(s32[17]{0:T(128)} %constant.156.clone) | copy-start | bytes 208
  108.2 56.3 %copy-start.15 = (f32[48,1024]{1,0:T(8,128)}, f32[48,1024]{1,0:T(8,128)S(1)}, u32[]{:S(2)}) copy-start(f32[48,1024]{1,0:T(8,128)S(1)} %collective-permute-done.15.refs_15_) | copy-start | bytes 589828
  109.9 54.6 %copy-start.16 = (f32[48,1024]{1,0:T(8,128)}, f32[48,1024]{1,0:T(8,128)S(1)}, u32[]{:S(2)}) copy-start(f32[48,1024]{1,0:T(8,128)S(1)} %collective-permute-done.16.refs_16_) | copy-start | bytes 589828
  150.5 11.5 %all-to-all-start.3 = ((f32[8,96,128]{2,1,0:T(8,128)}), f32[8,96,128]{2,1,0:T(8,128)S(1)}, u32[]{:S(2)}, u32[]{:S(2)}) async-start(f32[8,96,128]{2,1,0:T(8,128)} %broadcast_in_dim.8), calls=%async_computation.3 | async-start | bytes 786432 | tf_op jit(solution)/shard_map/all_to_all | solution.py:156
  (14 other events, 393.7 us)
where the time goes:
time: 195 us; the launch traced here: 191 us
  starting transfers between devices  78.5 us (40%)
  blocking collectives  57.4 us (29%)
  waiting for transfers between devices  29.2 us (15%)
  Pallas kernels  11.2 us (6%)
  matrix products  10.9 us (6%)
  other arithmetic  2 us (1%)
    ppermute x17, starting transfers between devices, moved(): lax.ppermute(value, axis, [(i, (i + steps) % count) for i in range(count)])  63.7 us
    ppermute x17, waiting for transfers between devices, moved(): lax.ppermute(value, axis, [(i, (i + steps) % count) for i in range(count)])  23.9 us
    all_to_all x1, blocking collectives, step_on_shards(): lax.all_to_all(jnp.broadcast_to(stats[None], (count_z,) + stats.shape), '...  21.7 us
    all_to_all x1, blocking collectives, step_on_shards(): scores = jnp.sum(lax.all_to_all(partial, PLANE, 0, 0, tiled=False), axis=0)  16.8 us
    all_to_all x1, blocking collectives, step_on_shards(): lax.all_to_all(out.reshape(owners, -1, width), OWNERS, 0, 0, tiled=False)  16.3 us
    dot_general x17, matrix products, place(): lax.dot_general(block, plane_refs, (((1,), (1,)), ((), ())), precision=HI...  10.9 us
    pallas_call x1, Pallas kernels, weighted(): pl.pallas_call(functools.partial(weighted_kernel, starts), out_shape=jax....  9.48 us
    all_to_all x1, starting transfers between devices, step_on_shards(): half = lax.all_to_all(pieces, ('x', 'core'), 0, 0, tiled=True)  9.17 us
  transfers between devices with their start and end apart: 19, of which 10 were waited for; matrix products, arithmetic and copies ran while one was open for 6% of the time, Pallas kernels for 1%

commit v1 on v0

--- a/solution.py
+++ b/solution.py
@@ -16,12 +16,6 @@
 def moved(value, axis, steps):
     count = lax.axis_size(axis)
     return lax.ppermute(value, axis, [(i, (i + steps) % count) for i in range(count)])
-
-
-def both(value, axis):
-    other = moved(value, axis, 1)
-    first = lax.axis_index(axis) == 0
-    return jnp.stack([jnp.where(first, value, other), jnp.where(first, other, value)])
 
 
 def cut_kernel(at_ref, images_ref, out_ref, sem):
@@ -44,39 +38,40 @@
     )(which.reshape(1).astype(jnp.int32), images)
 
 
+def halves(value):
+    high = value.astype(jnp.bfloat16)
+    return high, (value - high.astype(jnp.float32)).astype(jnp.bfloat16)
+
+
 def weighted_kernel(starts, at_ref, post_ref, *refs):
     count = len(starts)
-    blocks, (out_ref, held, order, sems) = refs[:count], refs[count:]
+    blocks, (out_ref, held, order, both, sems) = refs[:count], refs[count:]
+    tiles = sems.shape[0]
+    tile = out_ref.shape[1] // tiles
     copies = []
-    for k, block in enumerate(blocks):
-        copies.append(pltpu.make_async_copy(
-            block, held.at[pl.ds(starts[k], block.shape[0])], sems.at[k]))
-        copies[-1].start()
+    for t in range(tiles):
+        columns = pl.ds(t * tile, tile)
+        copies.append([pltpu.make_async_copy(
+            block.at[:, columns], held.at[pl.ds(starts[k], block.shape[0]), columns],
+            sems.at[t, k]) for k, block in enumerate(blocks)])
+        for copy in copies[-1]:
+            copy.start()
     for k, block in enumerate(blocks):
         size = block.shape[0]
         row = pl.multiple_of(at_ref[k], 8)
         order[starts[k]:starts[k] + size, :] = post_ref[pl.ds(row, size), :]
-    tile = 256
-    pieces = 3
-    part = held.shape[0] // pieces
-    waited = 0
-    for piece in range(pieces):
-        stop = (piece + 1) * part
-        while waited < count and starts[waited] < stop:
-            copies[waited].wait()
-            waited += 1
-        rows = pl.ds(piece * part, part)
-        post = order[rows, :].T
-
-        @pl.loop(0, out_ref.shape[1] // tile)
-        def _(t):
-            columns = pl.ds(pl.multiple_of(t * tile, tile), tile)
-            term = jnp.dot(post, held[rows, columns], precision=HIGHEST,
-                           preferred_element_type=jnp.float32)
-            if piece == 0:
-                out_ref[:, columns] = term
-            else:
-                out_ref[:, columns] += term
+    members = order.shape[1]
+    high, low = halves(order[...].T)
+    both[:members, :] = high
+    both[members:, :] = low
+    for t in range(tiles):
+        for copy in copies[t]:
+            copy.wait()
+        columns = pl.ds(t * tile, tile)
+        image_high, image_low = halves(held[:, columns])
+        wide = jnp.dot(both[...], image_high, preferred_element_type=jnp.float32)
+        rest = jnp.dot(both[:members, :], image_low, preferred_element_type=jnp.float32)
+        out_ref[:, columns] = wide[:members] + (wide[members:] + rest)
 
 
 def weighted(at, post, blocks):
@@ -94,9 +89,10 @@
         out_specs=pl.BlockSpec(memory_space=pltpu.VMEM),
         scratch_shapes=[pltpu.VMEM((images, width), jnp.float32),
                         pltpu.VMEM((images, refs), jnp.float32),
-                        pltpu.SemaphoreType.DMA((len(blocks),))],
+                        pltpu.VMEM((2 * refs, images), jnp.bfloat16),
+                        pltpu.SemaphoreType.DMA((4, len(blocks)))],
         cost_estimate=pl.CostEstimate(
-            flops=12 * images * refs * width, bytes_accessed=8 * images * width,
+            flops=6 * images * refs * width, bytes_accessed=8 * images * width,
             transcendentals=0),
         name="weighted",
     )(at, post, *blocks)
@@ -111,8 +107,10 @@
     rows = own.shape[0]
 
     pieces = references.reshape(references.shape[0], slices, width).transpose(1, 0, 2)
-    half = lax.all_to_all(pieces, ("x", "core"), 0, 0, tiled=True)
-    plane_refs = both(half, "yh").reshape(-1, width)
+    pieces = jnp.broadcast_to(pieces[None], (lax.axis_size("yh"),) + pieces.shape)
+    plane_refs = lax.all_to_all(
+        pieces.reshape((-1,) + pieces.shape[2:]), OWNERS, 0, 0, tiled=True)
+    plane_refs = plane_refs.reshape(-1, width)
     halfnorm = 0.5 * jnp.sum(plane_refs * plane_refs, axis=1)
 
     partial = jnp.zeros((count_z * rows, plane_refs.shape[0]), jnp.float32)

time: 195 us -> 197 us (1.010)
  waiting for transfers between devices: 29.2 us -> 33.4 us
  starting transfers between devices: 78.5 us -> 75.9 us
  Pallas kernels: 11.2 us -> 9.02 us
    ppermute x17 -> x16, waiting for transfers between devices: 23.9 us -> 28.1 us  [moved(): lax.ppermute(value, axis, [(i, (i + steps) % count) for i in range(count)])]
    ppermute x17 -> x16, starting transfers between devices: 63.7 us -> 61.1 us  [moved(): lax.ppermute(value, axis, [(i, (i + steps) % count) for i in range(count)])]
    pallas_call x1, Pallas kernels: 9.48 us -> 7.26 us  [weighted(): pl.pallas_call(functools.partial(weighted_kernel, starts), out_shape=jax....]
  transfers between devices with their start and end apart: 19 -> 18, of which waited for: 10 -> 10; matrix products, arithmetic and copies ran while one was open for 6% -> 6% of each run, Pallas kernels for 1% -> 1%
where the time goes in v1:
time: 197 us; the launch traced here: 193 us
  starting transfers between devices  75.9 us (39%)
  blocking collectives  57.3 us (29%)
  waiting for transfers between devices  33.4 us (17%)
  matrix products  11.9 us (6%)
  Pallas kernels  9.02 us (5%)
  local copies, waits for them, and re-layouts  2.85 us (1%)
    ppermute x16, starting transfers between devices, moved(): lax.ppermute(value, axis, [(i, (i + steps) % count) for i in range(count)])  61.1 us
    ppermute x16, waiting for transfers between devices, moved(): lax.ppermute(value, axis, [(i, (i + steps) % count) for i in range(count)])  28.1 us
    all_to_all x1, blocking collectives, step_on_shards(): lax.all_to_all(jnp.broadcast_to(stats[None], (count_z,) + stats.shape), '...  21.7 us
    all_to_all x1, blocking collectives, step_on_shards(): lax.all_to_all(out.reshape(owners, -1, width), OWNERS, 0, 0, tiled=False)  17 us
    all_to_all x1, blocking collectives, step_on_shards(): scores = jnp.sum(lax.all_to_all(partial, PLANE, 0, 0, tiled=False), axis=0)  15.9 us
    dot_general x17, matrix products, place(): lax.dot_general(block, plane_refs, (((1,), (1,)), ((), ())), precision=HI...  11.9 us
    all_to_all x1, starting transfers between devices, step_on_shards(): lax.all_to_all(pieces.reshape((-1,) + pieces.shape[2:]), OWNERS, 0, 0, ti...  9.22 us
    pallas_call x1, Pallas kernels, weighted(): pl.pallas_call(functools.partial(weighted_kernel, starts), out_shape=jax....  7.26 us
  transfers between devices with their start and end apart: 18, of which 10 were waited for; matrix products, arithmetic and copies ran while one was open for 6% of the time, Pallas kernels for 1%

profile of v1, /device:TPU:6, one launch (start us, length us, event | category | flops | bytes accessed | tf_op | source)
XLA Modules:
  0.0 193.1 jit_solution(11358396038613732383)
XLA Ops:
  1.8 9.2 %all-to-all-start = ((f32[16,8,1024]{2,1,0:T(8,128)}), f32[16,8,1024]{2,1,0:T(8,128)S(1)}, u32[]{:S(2)}, u32[]{:S(2)}) async-start(f32[16,8,1024]{2,1,0:T(8,128)} %bitcast.3), calls=%async_computation | async-start | bytes 1048576 | tf_op jit(solution)/shard_map/all_to_all | solution.py:111
  12.8 2.0 %collective-permute-start = (f32[96,1024]{1,0:T(8,128)}, f32[96,1024]{1,0:T(8,128)S(1)}, u32[]{:S(2)}, u32[]{:S(2)}) collective-permute-start(f32[96,1024]{1,0:T(8,128)} %cut.1.refs_0_), channel_id=1, source_target_pairs={{0,32},{32,64},{64,96},{96,128},{128,160},{160,192},{192,224},{224... | collective-permute-start | bytes 1179656 | tf_op jit(solution)/shard_map/ppermute | solution.py:18
  14.8 9.5 %collective-permute-start.1 = (f32[96,1024]{1,0:T(8,128)}, f32[96,1024]{1,0:T(8,128)S(1)}, u32[]{:S(2)}, u32[]{:S(2)}) collective-permute-start(f32[96,1024]{1,0:T(8,128)} %cut.1.refs_0_), channel_id=1, source_target_pairs={{0,480},{32,0},{64,32},{96,64},{128,96},{160,128},{192,160},{224,1... | collective-permute-start | bytes 1179656 | tf_op jit(solution)/shard_map/ppermute | solution.py:18
  24.7 7.3 %collective-permute-done.refs_1_ = f32[96,1024]{1,0:T(8,128)S(1)} collective-permute-done((f32[96,1024]{1,0:T(8,128)}, f32[96,1024]{1,0:T(8,128)S(1)}, u32[]{:S(2)}, u32[]{:S(2)}) %collective-permute-start) | collective-permute-done | bytes 393248 | tf_op jit(solution)/shard_map/ppermute | solution.py:18
  33.9 5.1 %collective-permute-start.3 = (f32[96,1024]{1,0:T(8,128)S(1)}, f32[96,1024]{1,0:T(8,128)S(1)}, u32[]{:S(2)}, u32[]{:S(2)}) collective-permute-start(f32[96,1024]{1,0:T(8,128)S(1)} %collective-permute-done.1.refs_2_), channel_id=1, source_target_pairs={{0,480},{32,0},{64,32},{96,64},{128,96},{160,128},{192,160},{224,1... | collective-permute-start | bytes 1179656 | tf_op jit(solution)/shard_map/ppermute | solution.py:18
  42.3 3.4 %collective-permute-done.2.refs_3_ = f32[96,1024]{1,0:T(8,128)S(1)} collective-permute-done((f32[96,1024]{1,0:T(8,128)S(1)}, f32[96,1024]{1,0:T(8,128)S(1)}, u32[]{:S(2)}, u32[]{:S(2)}) %collective-permute-start.2) | collective-permute-done | bytes 393248 | tf_op jit(solution)/shard_map/ppermute | solution.py:18
  47.6 5.1 %collective-permute-start.5 = (f32[96,1024]{1,0:T(8,128)S(1)}, f32[96,1024]{1,0:T(8,128)S(1)}, u32[]{:S(2)}, u32[]{:S(2)}) collective-permute-start(f32[96,1024]{1,0:T(8,128)S(1)} %collective-permute-done.3.refs_4_), channel_id=1, source_target_pairs={{0,480},{32,0},{64,32},{96,64},{128,96},{160,128},{192,160},{224,1... | collective-permute-start | bytes 1179656 | tf_op jit(solution)/shard_map/ppermute | solution.py:18
  54.0 4.4 %collective-permute-done.4.refs_5_ = f32[96,1024]{1,0:T(8,128)S(1)} collective-permute-done((f32[96,1024]{1,0:T(8,128)S(1)}, f32[96,1024]{1,0:T(8,128)S(1)}, u32[]{:S(2)}, u32[]{:S(2)}) %collective-permute-start.4) | collective-permute-done | bytes 393248 | tf_op jit(solution)/shard_map/ppermute | solution.py:18
  60.4 5.1 %collective-permute-start.7 = (f32[96,1024]{1,0:T(8,128)S(1)}, f32[96,1024]{1,0:T(8,128)S(1)}, u32[]{:S(2)}, u32[]{:S(2)}) collective-permute-start(f32[96,1024]{1,0:T(8,128)S(1)} %collective-permute-done.5.refs_6_), channel_id=1, source_target_pairs={{0,480},{32,0},{64,32},{96,64},{128,96},{160,128},{192,160},{224,1... | collective-permute-start | bytes 1179656 | tf_op jit(solution)/shard_map/ppermute | solution.py:18
  66.8 3.6 %collective-permute-done.6.refs_7_ = f32[96,1024]{1,0:T(8,128)S(1)} collective-permute-done((f32[96,1024]{1,0:T(8,128)S(1)}, f32[96,1024]{1,0:T(8,128)S(1)}, u32[]{:S(2)}, u32[]{:S(2)}) %collective-permute-start.6) | collective-permute-done | bytes 393248 | tf_op jit(solution)/shard_map/ppermute | solution.py:18
  72.3 5.1 %collective-permute-start.9 = (f32[96,1024]{1,0:T(8,128)S(1)}, f32[96,1024]{1,0:T(8,128)S(1)}, u32[]{:S(2)}, u32[]{:S(2)}) collective-permute-start(f32[96,1024]{1,0:T(8,128)S(1)} %collective-permute-done.7.refs_8_), channel_id=1, source_target_pairs={{0,480},{32,0},{64,32},{96,64},{128,96},{160,128},{192,160},{224,1... | collective-permute-start | bytes 1179656 | tf_op jit(solution)/shard_map/ppermute | solution.py:18
  78.8 2.7 %collective-permute-done.8.refs_9_ = f32[96,1024]{1,0:T(8,128)S(1)} collective-permute-done((f32[96,1024]{1,0:T(8,128)S(1)}, f32[96,1024]{1,0:T(8,128)S(1)}, u32[]{:S(2)}, u32[]{:S(2)}) %collective-permute-start.8) | collective-permute-done | bytes 393248 | tf_op jit(solution)/shard_map/ppermute | solution.py:18
  83.4 5.1 %collective-permute-start.11 = (f32[96,1024]{1,0:T(8,128)S(1)}, f32[96,1024]{1,0:T(8,128)S(1)}, u32[]{:S(2)}, u32[]{:S(2)}) collective-permute-start(f32[96,1024]{1,0:T(8,128)S(1)} %collective-permute-done.9.refs_10_), channel_id=1, source_target_pairs={{0,480},{32,0},{64,32},{96,64},{128,96},{160,128},{192,160},{224,1... | collective-permute-start | bytes 1179656 | tf_op jit(solution)/shard_map/ppermute | solution.py:18
  89.9 2.5 %collective-permute-done.10.refs_11_ = f32[96,1024]{1,0:T(8,128)S(1)} collective-permute-done((f32[96,1024]{1,0:T(8,128)S(1)}, f32[96,1024]{1,0:T(8,128)S(1)}, u32[]{:S(2)}, u32[]{:S(2)}) %collective-permute-start.10) | collective-permute-done | bytes 393248 | tf_op jit(solution)/shard_map/ppermute | solution.py:18
  94.3 5.1 %collective-permute-start.13 = (f32[96,1024]{1,0:T(8,128)S(1)}, f32[96,1024]{1,0:T(8,128)S(1)}, u32[]{:S(2)}, u32[]{:S(2)}) collective-permute-start(f32[96,1024]{1,0:T(8,128)S(1)} %collective-permute-done.11.refs_12_), channel_id=1, source_target_pairs={{0,480},{32,0},{64,32},{96,64},{128,96},{160,128},{192,160},{224,1... | collective-permute-start | bytes 1179656 | tf_op jit(solution)/shard_map/ppermute | solution.py:18
  100.7 2.9 %collective-permute-done.12.refs_13_ = f32[96,1024]{1,0:T(8,128)S(1)} collective-permute-done((f32[96,1024]{1,0:T(8,128)S(1)}, f32[96,1024]{1,0:T(8,128)S(1)}, u32[]{:S(2)}, u32[]{:S(2)}) %collective-permute-start.12) | collective-permute-done | bytes 393248 | tf_op jit(solution)/shard_map/ppermute | solution.py:18
  105.7 5.4 %collective-permute-start.15 = (f32[48,1024]{1,0:T(8,128)S(1)}, f32[48,1024]{1,0:T(8,128)S(1)}, u32[]{:S(2)}, u32[]{:S(2)}) collective-permute-start(f32[48,1024]{1,0:T(8,128)S(1)} %slice.18), channel_id=1, source_target_pairs={{0,480},{32,0},{64,32},{96,64},{128,96},{160,128},{192,160},{224,1... | collective-permute-start | bytes 589832 | tf_op jit(solution)/shard_map/ppermute | solution.py:18
  114.9 15.9 %all_to_all.25 = f32[16,96,128]{2,1,0:T(8,128)S(1)} all-to-all(f32[16,96,128]{2,1,0:T(8,128)S(1)} %bitcast.71), channel_id=1, replica_groups=mesh['z'=16,'yh'=2,'yl'=2,'x'=4,'core'=2] {'core','yl','x'}, dimensions={0} | all-to-all | bytes 1572864 | tf_op jit(solution)/shard_map/all_to_all | solution.py:142
  131.3 21.7 %all_to_all.26 = f32[16,2,96]{2,1,0:T(2,128)S(1)} all-to-all(f32[16,2,96]{2,1,0:T(2,128)S(1)} %broadcast_in_dim.10), channel_id=1, replica_groups=mesh['z'=16,'yh'=2,'yl'=2,'x'=4,'core'=2] {'z'}, dimensions={0} | all-to-all | bytes 24576 | tf_op jit(solution)/shard_map/all_to_all | solution.py:148
  153.9 5.6 %all-to-all-start.3 = ((f32[8,96,128]{2,1,0:T(8,128)}), f32[8,96,128]{2,1,0:T(8,128)S(1)}, u32[]{:S(2)}, u32[]{:S(2)}) async-start(f32[8,96,128]{2,1,0:T(8,128)} %broadcast_in_dim.11), calls=%async_computation.3 | async-start | bytes 786432 | tf_op jit(solution)/shard_map/all_to_all | solution.py:154
  160.2 5.3 %all-to-all-done.3 = f32[8,96,128]{2,1,0:T(8,128)S(1)} async-done(((f32[8,96,128]{2,1,0:T(8,128)}), f32[8,96,128]{2,1,0:T(8,128)S(1)}, u32[]{:S(2)}, u32[]{:S(2)}) %all-to-all-start.3) | async-done | bytes 393248 | tf_op jit(solution)/shard_map/all_to_all | solution.py:154
  165.4 2.7 %all-gather = f32[16,96,128]{2,1,0:T(8,128)} all-gather(f32[8,96,128]{2,1,0:T(8,128)S(1)} %all-to-all-done.3), channel_id=2, replica_groups=mesh['z'=16,'yh'=2,'yl'=2,'x'=4,'core'=2] {'core'}, dimensions={0}, use_global_device_ids=true | all-gather | bytes 1179648 | tf_op jit(solution)/shard_map/all_gather | solution.py:156
  168.1 7.3 %weighted.1 = f32[128,1024]{1,0:T(8,128)} custom-call(s32[17]{0:T(128)} %fusion.38.at_ref, f32[1536,128]{1,0:T(8,128)} %bitcast.70, f32[96,1024]{1,0:T(8,128)} %cut.1.refs_0_, f32[96,1024]{1,0:T(8,128)} %copy-done.2, f32[96,1024]{1,0:T(8,128)} %copy-done.3, f32[96,1024]{1,0:T(8,128)} %copy-done.4, f32[96,1024]{1,0:T(8,128)} %copy-done.5, ...), custom_call_target="tpu_custom_call" | custom-call | flops 1207959552 | bytes 12582912 | tf_op jit(solution)/shard_map/weighted/pallas_call | solution.py:83
  175.4 17.0 %all_to_all.27 = f32[16,8,1024]{2,1,0:T(8,128)S(1)} all-to-all(f32[16,8,1024]{2,1,0:T(8,128)} %bitcast.73), channel_id=1, replica_groups=mesh['z'=16,'yh'=2,'yl'=2,'x'=4,'core'=2] {'yh','x','core'}, dimensions={0} | all-to-all | bytes 1048576 | tf_op jit(solution)/shard_map/all_to_all | solution.py:162
  (91 shorter events, 33.0 us)
Async XLA Ops:
  1.8 37.3 %all-to-all-start = ((f32[16,8,1024]{2,1,0:T(8,128)}), f32[16,8,1024]{2,1,0:T(8,128)S(1)}, u32[]{:S(2)}, u32[]{:S(2)}) async-start(f32[16,8,1024]{2,1,0:T(8,128)} %bitcast.3), calls=%async_computation | async-start | bytes 1048576 | tf_op jit(solution)/shard_map/all_to_all | solution.py:111
  12.8 19.2 %collective-permute-start = (f32[96,1024]{1,0:T(8,128)}, f32[96,1024]{1,0:T(8,128)S(1)}, u32[]{:S(2)}, u32[]{:S(2)}) collective-permute-start(f32[96,1024]{1,0:T(8,128)} %cut.1.refs_0_), channel_id=1, source_target_pairs={{0,32},{32,64},{64,96},{96,128},{128,160},{160,192},{192,224},{224... | collective-permute-start | bytes 1179656 | tf_op jit(solution)/shard_map/ppermute | solution.py:18
  14.8 19.1 %collective-permute-start.1 = (f32[96,1024]{1,0:T(8,128)}, f32[96,1024]{1,0:T(8,128)S(1)}, u32[]{:S(2)}, u32[]{:S(2)}) collective-permute-start(f32[96,1024]{1,0:T(8,128)} %cut.1.refs_0_), channel_id=1, source_target_pairs={{0,480},{32,0},{64,32},{96,64},{128,96},{160,128},{192,160},{224,1... | collective-permute-start | bytes 1179656 | tf_op jit(solution)/shard_map/ppermute | solution.py:18
  32.0 13.7 %collective-permute-start.2 = (f32[96,1024]{1,0:T(8,128)S(1)}, f32[96,1024]{1,0:T(8,128)S(1)}, u32[]{:S(2)}, u32[]{:S(2)}) collective-permute-start(f32[96,1024]{1,0:T(8,128)S(1)} %collective-permute-done.refs_1_), channel_id=1, source_target_pairs={{0,32},{32,64},{64,96},{96,128},{128,160},{160,192},{192,224},{224... | collective-permute-start | bytes 1179656 | tf_op jit(solution)/shard_map/ppermute | solution.py:18
  33.9 13.6 %collective-permute-start.3 = (f32[96,1024]{1,0:T(8,128)S(1)}, f32[96,1024]{1,0:T(8,128)S(1)}, u32[]{:S(2)}, u32[]{:S(2)}) collective-permute-start(f32[96,1024]{1,0:T(8,128)S(1)} %collective-permute-done.1.refs_2_), channel_id=1, source_target_pairs={{0,480},{32,0},{64,32},{96,64},{128,96},{160,128},{192,160},{224,1... | collective-permute-start | bytes 1179656 | tf_op jit(solution)/shard_map/ppermute | solution.py:18
  45.7 43.5 %copy-start.4 = (f32[96,1024]{1,0:T(8,128)}, f32[96,1024]{1,0:T(8,128)S(1)}, u32[]{:S(2)}) copy-start(f32[96,1024]{1,0:T(8,128)S(1)} %collective-permute-done.2.refs_3_) | copy-start | bytes 1179652
  45.7 12.8 %collective-permute-start.4 = (f32[96,1024]{1,0:T(8,128)S(1)}, f32[96,1024]{1,0:T(8,128)S(1)}, u32[]{:S(2)}, u32[]{:S(2)}) collective-permute-start(f32[96,1024]{1,0:T(8,128)S(1)} %collective-permute-done.2.refs_3_), channel_id=1, source_target_pairs={{0,32},{32,64},{64,96},{96,128},{128,160},{160,192},{192,224},{224... | collective-permute-start | bytes 1179656 | tf_op jit(solution)/shard_map/ppermute | solution.py:18
  47.6 12.8 %collective-permute-start.5 = (f32[96,1024]{1,0:T(8,128)S(1)}, f32[96,1024]{1,0:T(8,128)S(1)}, u32[]{:S(2)}, u32[]{:S(2)}) collective-permute-start(f32[96,1024]{1,0:T(8,128)S(1)} %collective-permute-done.3.refs_4_), channel_id=1, source_target_pairs={{0,480},{32,0},{64,32},{96,64},{128,96},{160,128},{192,160},{224,1... | collective-permute-start | bytes 1179656 | tf_op jit(solution)/shard_map/ppermute | solution.py:18
  58.5 41.6 %copy-start.6 = (f32[96,1024]{1,0:T(8,128)}, f32[96,1024]{1,0:T(8,128)S(1)}, u32[]{:S(2)}) copy-start(f32[96,1024]{1,0:T(8,128)S(1)} %collective-permute-done.4.refs_5_) | copy-start | bytes 1179652
  58.5 11.9 %collective-permute-start.6 = (f32[96,1024]{1,0:T(8,128)S(1)}, f32[96,1024]{1,0:T(8,128)S(1)}, u32[]{:S(2)}, u32[]{:S(2)}) collective-permute-start(f32[96,1024]{1,0:T(8,128)S(1)} %collective-permute-done.4.refs_5_), channel_id=1, source_target_pairs={{0,32},{32,64},{64,96},{96,128},{128,160},{160,192},{192,224},{224... | collective-permute-start | bytes 1179656 | tf_op jit(solution)/shard_map/ppermute | solution.py:18
  60.4 11.9 %collective-permute-start.7 = (f32[96,1024]{1,0:T(8,128)S(1)}, f32[96,1024]{1,0:T(8,128)S(1)}, u32[]{:S(2)}, u32[]{:S(2)}) collective-permute-start(f32[96,1024]{1,0:T(8,128)S(1)} %collective-permute-done.5.refs_6_), channel_id=1, source_target_pairs={{0,480},{32,0},{64,32},{96,64},{128,96},{160,128},{192,160},{224,1... | collective-permute-start | bytes 1179656 | tf_op jit(solution)/shard_map/ppermute | solution.py:18
  70.4 11.1 %collective-permute-start.8 = (f32[96,1024]{1,0:T(8,128)S(1)}, f32[96,1024]{1,0:T(8,128)S(1)}, u32[]{:S(2)}, u32[]{:S(2)}) collective-permute-start(f32[96,1024]{1,0:T(8,128)S(1)} %collective-permute-done.6.refs_7_), channel_id=1, source_target_pairs={{0,32},{32,64},{64,96},{96,128},{128,160},{160,192},{192,224},{224... | collective-permute-start | bytes 1179656 | tf_op jit(solution)/shard_map/ppermute | solution.py:18
  72.3 11.1 %collective-permute-start.9 = (f32[96,1024]{1,0:T(8,128)S(1)}, f32[96,1024]{1,0:T(8,128)S(1)}, u32[]{:S(2)}, u32[]{:S(2)}) collective-permute-start(f32[96,1024]{1,0:T(8,128)S(1)} %collective-permute-done.7.refs_8_), channel_id=1, source_target_pairs={{0,480},{32,0},{64,32},{96,64},{128,96},{160,128},{192,160},{224,1... | collective-permute-start | bytes 1179656 | tf_op jit(solution)/shard_map/ppermute | solution.py:18
  81.5 10.9 %collective-permute-start.10 = (f32[96,1024]{1,0:T(8,128)S(1)}, f32[96,1024]{1,0:T(8,128)S(1)}, u32[]{:S(2)}, u32[]{:S(2)}) collective-permute-start(f32[96,1024]{1,0:T(8,128)S(1)} %collective-permute-done.8.refs_9_), channel_id=1, source_target_pairs={{0,32},{32,64},{64,96},{96,128},{128,160},{160,192},{192,224},{224... | collective-permute-start | bytes 1179656 | tf_op jit(solution)/shard_map/ppermute | solution.py:18
  83.4 10.9 %collective-permute-start.11 = (f32[96,1024]{1,0:T(8,128)S(1)}, f32[96,1024]{1,0:T(8,128)S(1)}, u32[]{:S(2)}, u32[]{:S(2)}) collective-permute-start(f32[96,1024]{1,0:T(8,128)S(1)} %collective-permute-done.9.refs_10_), channel_id=1, source_target_pairs={{0,480},{32,0},{64,32},{96,64},{128,96},{160,128},{192,160},{224,1... | collective-permute-start | bytes 1179656 | tf_op jit(solution)/shard_map/ppermute | solution.py:18
  92.4 11.3 %collective-permute-start.12 = (f32[96,1024]{1,0:T(8,128)S(1)}, f32[96,1024]{1,0:T(8,128)S(1)}, u32[]{:S(2)}, u32[]{:S(2)}) collective-permute-start(f32[96,1024]{1,0:T(8,128)S(1)} %collective-permute-done.10.refs_11_), channel_id=1, source_target_pairs={{0,32},{32,64},{64,96},{96,128},{128,160},{160,192},{192,224},{224... | collective-permute-start | bytes 1179656 | tf_op jit(solution)/shard_map/ppermute | solution.py:18
  94.3 11.3 %collective-permute-start.13 = (f32[96,1024]{1,0:T(8,128)S(1)}, f32[96,1024]{1,0:T(8,128)S(1)}, u32[]{:S(2)}, u32[]{:S(2)}) collective-permute-start(f32[96,1024]{1,0:T(8,128)S(1)} %collective-permute-done.11.refs_12_), channel_id=1, source_target_pairs={{0,480},{32,0},{64,32},{96,64},{128,96},{160,128},{192,160},{224,1... | collective-permute-start | bytes 1179656 | tf_op jit(solution)/shard_map/ppermute | solution.py:18
  103.7 8.8 %collective-permute-start.14 = (f32[48,1024]{1,0:T(8,128)S(1)}, f32[48,1024]{1,0:T(8,128)S(1)}, u32[]{:S(2)}, u32[]{:S(2)}) collective-permute-start(f32[48,1024]{1,0:T(8,128)S(1)} %slice.17), channel_id=1, source_target_pairs={{0,32},{32,64},{64,96},{96,128},{128,160},{160,192},{192,224},{224... | collective-permute-start | bytes 589832 | tf_op jit(solution)/shard_map/ppermute | solution.py:18
  105.7 8.6 %collective-permute-start.15 = (f32[48,1024]{1,0:T(8,128)S(1)}, f32[48,1024]{1,0:T(8,128)S(1)}, u32[]{:S(2)}, u32[]{:S(2)}) collective-permute-start(f32[48,1024]{1,0:T(8,128)S(1)} %slice.18), channel_id=1, source_target_pairs={{0,480},{32,0},{64,32},{96,64},{128,96},{160,128},{192,160},{224,1... | collective-permute-start | bytes 589832 | tf_op jit(solution)/shard_map/ppermute | solution.py:18
  111.7 47.8 %copy-start.16 = (s32[17]{0:T(128)S(1)}, s32[17]{0:T(128)}, u32[]{:S(2)}) copy-start(s32[17]{0:T(128)} %constant.152.clone) | copy-start | bytes 208
  111.7 47.8 %copy-start.17 = (s32[17]{0:T(128)S(1)}, s32[17]{0:T(128)}, u32[]{:S(2)}) copy-start(s32[17]{0:T(128)} %constant.153.clone) | copy-start | bytes 208
  112.5 55.6 %copy-start.14 = (f32[48,1024]{1,0:T(8,128)}, f32[48,1024]{1,0:T(8,128)S(1)}, u32[]{:S(2)}) copy-start(f32[48,1024]{1,0:T(8,128)S(1)} %collective-permute-done.14.refs_15_) | copy-start | bytes 589828
  114.2 53.8 %copy-start.15 = (f32[48,1024]{1,0:T(8,128)}, f32[48,1024]{1,0:T(8,128)S(1)}, u32[]{:S(2)}) copy-start(f32[48,1024]{1,0:T(8,128)S(1)} %collective-permute-done.15.refs_16_) | copy-start | bytes 589828
  153.9 11.5 %all-to-all-start.3 = ((f32[8,96,128]{2,1,0:T(8,128)}), f32[8,96,128]{2,1,0:T(8,128)S(1)}, u32[]{:S(2)}, u32[]{:S(2)}) async-start(f32[8,96,128]{2,1,0:T(8,128)} %broadcast_in_dim.11), calls=%async_computation.3 | async-start | bytes 786432 | tf_op jit(solution)/shard_map/all_to_all | solution.py:154
  (12 other events, 350.6 us)

commit v2 on v1

--- a/solution.py
+++ b/solution.py
@@ -43,59 +43,74 @@
     return high, (value - high.astype(jnp.float32)).astype(jnp.bfloat16)
 
 
-def weighted_kernel(starts, at_ref, post_ref, *refs):
+def split_kernel(starts, at_ref, *refs):
     count = len(starts)
-    blocks, (out_ref, held, order, both, sems) = refs[:count], refs[count:]
-    tiles = sems.shape[0]
-    tile = out_ref.shape[1] // tiles
+    blocks, (high_ref, low_ref, held, sems) = refs[:count], refs[count:]
     copies = []
-    for t in range(tiles):
-        columns = pl.ds(t * tile, tile)
-        copies.append([pltpu.make_async_copy(
-            block.at[:, columns], held.at[pl.ds(starts[k], block.shape[0]), columns],
-            sems.at[t, k]) for k, block in enumerate(blocks)])
-        for copy in copies[-1]:
-            copy.start()
+    for k, block in enumerate(blocks):
+        copies.append(pltpu.make_async_copy(
+            block, held.at[pl.ds(starts[k], block.shape[0])], sems.at[k]))
+        copies[-1].start()
     for k, block in enumerate(blocks):
         size = block.shape[0]
-        row = pl.multiple_of(at_ref[k], 8)
-        order[starts[k]:starts[k] + size, :] = post_ref[pl.ds(row, size), :]
-    members = order.shape[1]
-    high, low = halves(order[...].T)
-    both[:members, :] = high
-    both[members:, :] = low
-    for t in range(tiles):
-        for copy in copies[t]:
-            copy.wait()
-        columns = pl.ds(t * tile, tile)
-        image_high, image_low = halves(held[:, columns])
-        wide = jnp.dot(both[...], image_high, preferred_element_type=jnp.float32)
-        rest = jnp.dot(both[:members, :], image_low, preferred_element_type=jnp.float32)
-        out_ref[:, columns] = wide[:members] + (wide[members:] + rest)
+        rows = pl.ds(pl.multiple_of(at_ref[k], 16), size)
+        copies[k].wait()
+        high_ref[rows, :], low_ref[rows, :] = halves(held[starts[k]:starts[k] + size, :])
 
 
-def weighted(at, post, blocks):
-    images, refs = post.shape
+def split(at, blocks):
     width = blocks[0].shape[1]
     starts = [0]
-    for block in blocks[:-1]:
+    for block in blocks:
         starts.append(starts[-1] + block.shape[0])
+    images = starts.pop()
+    half = jax.ShapeDtypeStruct((images, width), jnp.bfloat16)
     return pl.pallas_call(
-        functools.partial(weighted_kernel, starts),
+        functools.partial(split_kernel, starts),
+        out_shape=(half, half),
+        in_specs=[pl.BlockSpec(memory_space=pltpu.SMEM)]
+        + [pl.BlockSpec(memory_space=pl.ANY)] * len(blocks),
+        out_specs=(pl.BlockSpec(memory_space=pltpu.VMEM),) * 2,
+        scratch_shapes=[pltpu.VMEM((images, width), jnp.float32),
+                        pltpu.SemaphoreType.DMA((len(blocks),))],
+        cost_estimate=pl.CostEstimate(
+            flops=4 * images * width, bytes_accessed=8 * images * width, transcendentals=0),
+        name="split",
+    )(at, *blocks)
+
+
+def weighted_kernel(post_ref, high_ref, low_ref, out_ref, both):
+    members = post_ref.shape[1]
+
+    @pl.when(pl.program_id(0) == 0)
+    def _():
+        high, low = halves(post_ref[...].T)
+        both[:members, :] = high
+        both[members:, :] = low
+
+    wide = jnp.dot(both[...], high_ref[...], preferred_element_type=jnp.float32)
+    rest = jnp.dot(both[:members, :], low_ref[...], preferred_element_type=jnp.float32)
+    out_ref[...] = wide[:members] + (wide[members:] + rest)
+
+
+def weighted(post, high, low):
+    images, refs = post.shape
+    width = high.shape[1]
+    tile = 256
+    return pl.pallas_call(
+        weighted_kernel,
         out_shape=jax.ShapeDtypeStruct((refs, width), jnp.float32),
-        in_specs=[pl.BlockSpec(memory_space=pltpu.SMEM),
-                  pl.BlockSpec(memory_space=pltpu.VMEM)]
-        + [pl.BlockSpec(memory_space=pl.ANY)] * len(blocks),
-        out_specs=pl.BlockSpec(memory_space=pltpu.VMEM),
-        scratch_shapes=[pltpu.VMEM((images, width), jnp.float32),
-                        pltpu.VMEM((images, refs), jnp.float32),
-                        pltpu.VMEM((2 * refs, images), jnp.bfloat16),
-                        pltpu.SemaphoreType.DMA((4, len(blocks)))],
+        grid=(width // tile,),
+        in_specs=[pl.BlockSpec((images, refs), lambda t: (0, 0)),
+                  pl.BlockSpec((images, tile), lambda t: (0, t)),
+                  pl.BlockSpec((images, tile), lambda t: (0, t))],
+        out_specs=pl.BlockSpec((refs, tile), lambda t: (0, t)),
+        scratch_shapes=[pltpu.VMEM((2 * refs, images), jnp.bfloat16)],
         cost_estimate=pl.CostEstimate(
-            flops=6 * images * refs * width, bytes_accessed=8 * images * width,
+            flops=6 * images * refs * width, bytes_accessed=4 * images * width,
             transcendentals=0),
         name="weighted",
-    )(at, post, *blocks)
+    )(post, high, low)
 
 
 def step_on_shards(images, references):
@@ -139,7 +154,10 @@
         partial = place(partial, left, step, middle)
 
     partial = partial.reshape(count_z, rows, -1)
-    scores = jnp.sum(lax.all_to_all(partial, PLANE, 0, 0, tiled=False), axis=0)
+    at = (here + jnp.array(offsets, jnp.int32)) % count_z * rows + jnp.array(firsts, jnp.int32)
+    high, low = split(at, blocks)
+    everything = lax.all_to_all(partial, PLANE, 0, 0, tiled=False)
+    scores = jnp.sum(everything, axis=0)
 
     largest = jnp.max(scores, axis=1)
     expon = jnp.exp(scores - largest[:, None])
@@ -155,8 +173,7 @@
         jnp.broadcast_to(post[None], (chips,) + post.shape), ("yl", "x"), 0, 0, tiled=False)
     post = lax.all_gather(spread, "core").reshape(-1, post.shape[1])
 
-    at = (here + jnp.array(offsets, jnp.int32)) % count_z * rows + jnp.array(firsts, jnp.int32)
-    out = weighted(at, post, blocks)
+    out = weighted(post, high, low)
 
     owners = lax.axis_size("yh") * slices
     back = lax.all_to_all(out.reshape(owners, -1, width), OWNERS, 0, 0, tiled=False)

time: 197 us -> 197 us (level)
  Pallas kernels: 9.02 us -> 14 us
  waiting for transfers between devices: 33.4 us -> 29 us
  blocking collectives: 57.3 us -> 54 us
  starting transfers between devices: 75.9 us -> 78.8 us
    all_to_all x1, waiting for transfers between devices: 5.26 us -> 0.01 us  [step_on_shards(): lax.all_to_all(jnp.broadcast_to(post[None], (chips,) + post.shape), ('yl'...]
    pallas_call x1 -> x2, Pallas kernels: 7.26 us -> 12.2 us  [the longest x1 6.25 us: split(): pl.pallas_call(functools.partial(split_kernel, starts), out_shape=(half,...]
    all_to_all x1, blocking collectives: 21.7 us -> 18.3 us  [step_on_shards(): lax.all_to_all(jnp.broadcast_to(stats[None], (count_z,) + stats.shape), '...]
    ppermute x16, starting transfers between devices: 61.1 us -> 64 us  [moved(): lax.ppermute(value, axis, [(i, (i + steps) % count) for i in range(count)])]
  transfers between devices with their start and end apart: 18 -> 18, of which waited for: 10 -> 10; matrix products, arithmetic and copies ran while one was open for 6% -> 6% of each run, Pallas kernels for 1% -> 4%
where the time goes in v2:
time: 197 us; the launch traced here: 193 us
  starting transfers between devices  78.8 us (40%)
  blocking collectives  54 us (27%)
  waiting for transfers between devices  29 us (15%)
  Pallas kernels  14 us (7%)
  matrix products  11.9 us (6%)
  local copies, waits for them, and re-layouts  2.86 us (1%)
    ppermute x16, starting transfers between devices, moved(): lax.ppermute(value, axis, [(i, (i + steps) % count) for i in range(count)])  64 us
    ppermute x16, waiting for transfers between devices, moved(): lax.ppermute(value, axis, [(i, (i + steps) % count) for i in range(count)])  29 us
    all_to_all x1, blocking collectives, step_on_shards(): lax.all_to_all(jnp.broadcast_to(stats[None], (count_z,) + stats.shape), '...  18.3 us
    all_to_all x1, blocking collectives, step_on_shards(): lax.all_to_all(out.reshape(owners, -1, width), OWNERS, 0, 0, tiled=False)  17.2 us
    all_to_all x1, blocking collectives, step_on_shards(): everything = lax.all_to_all(partial, PLANE, 0, 0, tiled=False)  15.9 us
    dot_general x17, matrix products, place(): lax.dot_general(block, plane_refs, (((1,), (1,)), ((), ())), precision=HI...  11.9 us
    all_to_all x1, starting transfers between devices, step_on_shards(): lax.all_to_all(pieces.reshape((-1,) + pieces.shape[2:]), OWNERS, 0, 0, ti...  9.22 us
    pallas_call x1, Pallas kernels, split(): pl.pallas_call(functools.partial(split_kernel, starts), out_shape=(half,...  6.25 us
  transfers between devices with their start and end apart: 18, of which 10 were waited for; matrix products, arithmetic and copies ran while one was open for 6% of the time, Pallas kernels for 4%

profile of v2, /device:TPU:6, one launch (start us, length us, event | category | flops | bytes accessed | tf_op | source)
XLA Modules:
  0.0 193.2 jit_solution(14270676328830801312)
XLA Ops:
  1.8 9.2 %all-to-all-start = ((f32[16,8,1024]{2,1,0:T(8,128)}), f32[16,8,1024]{2,1,0:T(8,128)S(1)}, u32[]{:S(2)}, u32[]{:S(2)}) async-start(f32[16,8,1024]{2,1,0:T(8,128)} %bitcast.3), calls=%async_computation | async-start | bytes 1048576 | tf_op jit(solution)/shard_map/all_to_all | solution.py:126
  12.8 9.6 %collective-permute-start.1 = (f32[96,1024]{1,0:T(8,128)}, f32[96,1024]{1,0:T(8,128)S(1)}, u32[]{:S(2)}, u32[]{:S(2)}) collective-permute-start(f32[96,1024]{1,0:T(8,128)} %cut.1.refs_0_), channel_id=1, source_target_pairs={{0,480},{32,0},{64,32},{96,64},{128,96},{160,128},{192,160},{224,1... | collective-permute-start | bytes 1179656 | tf_op jit(solution)/shard_map/ppermute | solution.py:18
  24.7 6.7 %collective-permute-done.1.refs_2_ = f32[96,1024]{1,0:T(8,128)S(1)} collective-permute-done((f32[96,1024]{1,0:T(8,128)}, f32[96,1024]{1,0:T(8,128)S(1)}, u32[]{:S(2)}, u32[]{:S(2)}) %collective-permute-start.1) | collective-permute-done | bytes 393248 | tf_op jit(solution)/shard_map/ppermute | solution.py:18
  31.4 5.5 %collective-permute-start.3 = (f32[96,1024]{1,0:T(8,128)S(1)}, f32[96,1024]{1,0:T(8,128)S(1)}, u32[]{:S(2)}, u32[]{:S(2)}) collective-permute-start(f32[96,1024]{1,0:T(8,128)S(1)} %collective-permute-done.1.refs_2_), channel_id=1, source_target_pairs={{0,480},{32,0},{64,32},{96,64},{128,96},{160,128},{192,160},{224,1... | collective-permute-start | bytes 1179656 | tf_op jit(solution)/shard_map/ppermute | solution.py:18
  42.0 2.6 %collective-permute-done.3.refs_4_ = f32[96,1024]{1,0:T(8,128)S(1)} collective-permute-done((f32[96,1024]{1,0:T(8,128)S(1)}, f32[96,1024]{1,0:T(8,128)S(1)}, u32[]{:S(2)}, u32[]{:S(2)}) %collective-permute-start.3) | collective-permute-done | bytes 393248 | tf_op jit(solution)/shard_map/ppermute | solution.py:18
  44.6 5.6 %collective-permute-start.5 = (f32[96,1024]{1,0:T(8,128)S(1)}, f32[96,1024]{1,0:T(8,128)S(1)}, u32[]{:S(2)}, u32[]{:S(2)}) collective-permute-start(f32[96,1024]{1,0:T(8,128)S(1)} %collective-permute-done.3.refs_4_), channel_id=1, source_target_pairs={{0,480},{32,0},{64,32},{96,64},{128,96},{160,128},{192,160},{224,1... | collective-permute-start | bytes 1179656 | tf_op jit(solution)/shard_map/ppermute | solution.py:18
  53.4 3.7 %collective-permute-done.5.refs_6_ = f32[96,1024]{1,0:T(8,128)S(1)} collective-permute-done((f32[96,1024]{1,0:T(8,128)S(1)}, f32[96,1024]{1,0:T(8,128)S(1)}, u32[]{:S(2)}, u32[]{:S(2)}) %collective-permute-start.5) | collective-permute-done | bytes 393248 | tf_op jit(solution)/shard_map/ppermute | solution.py:18
  57.1 5.6 %collective-permute-start.7 = (f32[96,1024]{1,0:T(8,128)S(1)}, f32[96,1024]{1,0:T(8,128)S(1)}, u32[]{:S(2)}, u32[]{:S(2)}) collective-permute-start(f32[96,1024]{1,0:T(8,128)S(1)} %collective-permute-done.5.refs_6_), channel_id=1, source_target_pairs={{0,480},{32,0},{64,32},{96,64},{128,96},{160,128},{192,160},{224,1... | collective-permute-start | bytes 1179656 | tf_op jit(solution)/shard_map/ppermute | solution.py:18
  66.0 2.8 %collective-permute-done.7.refs_8_ = f32[96,1024]{1,0:T(8,128)S(1)} collective-permute-done((f32[96,1024]{1,0:T(8,128)S(1)}, f32[96,1024]{1,0:T(8,128)S(1)}, u32[]{:S(2)}, u32[]{:S(2)}) %collective-permute-start.7) | collective-permute-done | bytes 393248 | tf_op jit(solution)/shard_map/ppermute | solution.py:18
  68.8 5.6 %collective-permute-start.9 = (f32[96,1024]{1,0:T(8,128)S(1)}, f32[96,1024]{1,0:T(8,128)S(1)}, u32[]{:S(2)}, u32[]{:S(2)}) collective-permute-start(f32[96,1024]{1,0:T(8,128)S(1)} %collective-permute-done.7.refs_8_), channel_id=1, source_target_pairs={{0,480},{32,0},{64,32},{96,64},{128,96},{160,128},{192,160},{224,1... | collective-permute-start | bytes 1179656 | tf_op jit(solution)/shard_map/ppermute | solution.py:18
  77.6 2.0 %collective-permute-done.9.refs_10_ = f32[96,1024]{1,0:T(8,128)S(1)} collective-permute-done((f32[96,1024]{1,0:T(8,128)S(1)}, f32[96,1024]{1,0:T(8,128)S(1)}, u32[]{:S(2)}, u32[]{:S(2)}) %collective-permute-start.9) | collective-permute-done | bytes 393248 | tf_op jit(solution)/shard_map/ppermute | solution.py:18
  79.7 5.6 %collective-permute-start.11 = (f32[96,1024]{1,0:T(8,128)S(1)}, f32[96,1024]{1,0:T(8,128)S(1)}, u32[]{:S(2)}, u32[]{:S(2)}) collective-permute-start(f32[96,1024]{1,0:T(8,128)S(1)} %collective-permute-done.9.refs_10_), channel_id=1, source_target_pairs={{0,480},{32,0},{64,32},{96,64},{128,96},{160,128},{192,160},{224,1... | collective-permute-start | bytes 1179656 | tf_op jit(solution)/shard_map/ppermute | solution.py:18
  88.5 2.0 %collective-permute-done.11.refs_12_ = f32[96,1024]{1,0:T(8,128)S(1)} collective-permute-done((f32[96,1024]{1,0:T(8,128)S(1)}, f32[96,1024]{1,0:T(8,128)S(1)}, u32[]{:S(2)}, u32[]{:S(2)}) %collective-permute-start.11) | collective-permute-done | bytes 393248 | tf_op jit(solution)/shard_map/ppermute | solution.py:18
  90.5 5.6 %collective-permute-start.13 = (f32[96,1024]{1,0:T(8,128)S(1)}, f32[96,1024]{1,0:T(8,128)S(1)}, u32[]{:S(2)}, u32[]{:S(2)}) collective-permute-start(f32[96,1024]{1,0:T(8,128)S(1)} %collective-permute-done.11.refs_12_), channel_id=1, source_target_pairs={{0,480},{32,0},{64,32},{96,64},{128,96},{160,128},{192,160},{224,1... | collective-permute-start | bytes 1179656 | tf_op jit(solution)/shard_map/ppermute | solution.py:18
  99.6 2.9 %collective-permute-done.13.refs_14_ = f32[96,1024]{1,0:T(8,128)S(1)} collective-permute-done((f32[96,1024]{1,0:T(8,128)S(1)}, f32[96,1024]{1,0:T(8,128)S(1)}, u32[]{:S(2)}, u32[]{:S(2)}) %collective-permute-start.13) | collective-permute-done | bytes 393248 | tf_op jit(solution)/shard_map/ppermute | solution.py:18
  102.5 5.6 %collective-permute-start.15 = (f32[48,1024]{1,0:T(8,128)S(1)}, f32[48,1024]{1,0:T(8,128)S(1)}, u32[]{:S(2)}, u32[]{:S(2)}) collective-permute-start(f32[48,1024]{1,0:T(8,128)S(1)} %slice.18), channel_id=1, source_target_pairs={{0,480},{32,0},{64,32},{96,64},{128,96},{160,128},{192,160},{224,1... | collective-permute-start | bytes 589832 | tf_op jit(solution)/shard_map/ppermute | solution.py:18
  111.8 5.5 %collective-permute-done.14.refs_15_ = f32[48,1024]{1,0:T(8,128)S(1)} collective-permute-done((f32[48,1024]{1,0:T(8,128)S(1)}, f32[48,1024]{1,0:T(8,128)S(1)}, u32[]{:S(2)}, u32[]{:S(2)}) %collective-permute-start.14) | collective-permute-done | bytes 196640 | tf_op jit(solution)/shard_map/ppermute | solution.py:18
  118.7 15.9 %all_to_all.25 = f32[16,96,128]{2,1,0:T(8,128)S(1)} all-to-all(f32[16,96,128]{2,1,0:T(8,128)S(1)} %bitcast.71), channel_id=1, replica_groups=mesh['z'=16,'yh'=2,'yl'=2,'x'=4,'core'=2] {'core','yl','x'}, dimensions={0} | all-to-all | bytes 1572864 | tf_op jit(solution)/shard_map/all_to_all | solution.py:159
  135.0 18.3 %all_to_all.26 = f32[16,2,96]{2,1,0:T(2,128)S(1)} all-to-all(f32[16,2,96]{2,1,0:T(2,128)S(1)} %broadcast_in_dim.10), channel_id=1, replica_groups=mesh['z'=16,'yh'=2,'yl'=2,'x'=4,'core'=2] {'z'}, dimensions={0} | all-to-all | bytes 24576 | tf_op jit(solution)/shard_map/all_to_all | solution.py:166
  154.3 5.6 %all-to-all-start.3 = ((f32[8,96,128]{2,1,0:T(8,128)}), f32[8,96,128]{2,1,0:T(8,128)S(1)}, u32[]{:S(2)}, u32[]{:S(2)}) async-start(f32[8,96,128]{2,1,0:T(8,128)} %broadcast_in_dim.11), calls=%async_computation.3 | async-start | bytes 786432 | tf_op jit(solution)/shard_map/all_to_all | solution.py:172
  160.6 6.2 %split.1 = (bf16[1536,1024]{1,0:T(8,128)(2,1)}, bf16[1536,1024]{1,0:T(8,128)(2,1)}) custom-call(s32[17]{0:T(128)} %fusion.38.at_ref, f32[96,1024]{1,0:T(8,128)} %cut.1.refs_0_, f32[96,1024]{1,0:T(8,128)} %copy-done.3, f32[96,1024]{1,0:T(8,128)} %copy-done.2, f32[96,1024]{1,0:T(8,128)} %copy-done.5, f32[96,1024]{1,0:T(8,128)} %copy-done.4, ...), custom_call_target="tpu_custom_call" | custom-call | flops 6291456 | bytes 12582912 | tf_op jit(solution)/shard_map/split/pallas_call | solution.py:68
  166.8 2.5 %all-gather = f32[16,96,128]{2,1,0:T(8,128)} all-gather(f32[8,96,128]{2,1,0:T(8,128)S(1)} %all-to-all-done.3), channel_id=2, replica_groups=mesh['z'=16,'yh'=2,'yl'=2,'x'=4,'core'=2] {'core'}, dimensions={0}, use_global_device_ids=true | all-gather | bytes 1179648 | tf_op jit(solution)/shard_map/all_gather | solution.py:174
  169.3 5.9 %weighted.1 = f32[128,1024]{1,0:T(8,128)} custom-call(f32[1536,128]{1,0:T(8,128)} %bitcast.70, bf16[1536,1024]{1,0:T(8,128)(2,1)} %get-tuple-element.7.high_ref, bf16[1536,1024]{1,0:T(8,128)(2,1)} %get-tuple-element.8.low_ref), custom_call_target="tpu_custom_call" | custom-call | flops 1207959552 | bytes 6291456 | tf_op jit(solution)/shard_map/weighted/pallas_call | solution.py:100
  175.3 17.2 %all_to_all.27 = f32[16,8,1024]{2,1,0:T(8,128)S(1)} all-to-all(f32[16,8,1024]{2,1,0:T(8,128)} %bitcast.73), channel_id=1, replica_groups=mesh['z'=16,'yh'=2,'yl'=2,'x'=4,'core'=2] {'yh','x','core'}, dimensions={0} | all-to-all | bytes 1048576 | tf_op jit(solution)/shard_map/all_to_all | solution.py:179
  (92 shorter events, 34.4 us)
Async XLA Ops:
  1.8 37.0 %all-to-all-start = ((f32[16,8,1024]{2,1,0:T(8,128)}), f32[16,8,1024]{2,1,0:T(8,128)S(1)}, u32[]{:S(2)}, u32[]{:S(2)}) async-start(f32[16,8,1024]{2,1,0:T(8,128)} %bitcast.3), calls=%async_computation | async-start | bytes 1048576 | tf_op jit(solution)/shard_map/all_to_all | solution.py:126
  12.8 18.6 %collective-permute-start.1 = (f32[96,1024]{1,0:T(8,128)}, f32[96,1024]{1,0:T(8,128)S(1)}, u32[]{:S(2)}, u32[]{:S(2)}) collective-permute-start(f32[96,1024]{1,0:T(8,128)} %cut.1.refs_0_), channel_id=1, source_target_pairs={{0,480},{32,0},{64,32},{96,64},{128,96},{160,128},{192,160},{224,1... | collective-permute-start | bytes 1179656 | tf_op jit(solution)/shard_map/ppermute | solution.py:18
  22.4 14.4 %collective-permute-start = (f32[96,1024]{1,0:T(8,128)}, f32[96,1024]{1,0:T(8,128)S(1)}, u32[]{:S(2)}, u32[]{:S(2)}) collective-permute-start(f32[96,1024]{1,0:T(8,128)} %cut.1.refs_0_), channel_id=1, source_target_pairs={{0,32},{32,64},{64,96},{96,128},{128,160},{160,192},{192,224},{224... | collective-permute-start | bytes 1179656 | tf_op jit(solution)/shard_map/ppermute | solution.py:18
  31.4 13.3 %collective-permute-start.3 = (f32[96,1024]{1,0:T(8,128)S(1)}, f32[96,1024]{1,0:T(8,128)S(1)}, u32[]{:S(2)}, u32[]{:S(2)}) collective-permute-start(f32[96,1024]{1,0:T(8,128)S(1)} %collective-permute-done.1.refs_2_), channel_id=1, source_target_pairs={{0,480},{32,0},{64,32},{96,64},{128,96},{160,128},{192,160},{224,1... | collective-permute-start | bytes 1179656 | tf_op jit(solution)/shard_map/ppermute | solution.py:18
  36.9 13.4 %collective-permute-start.2 = (f32[96,1024]{1,0:T(8,128)S(1)}, f32[96,1024]{1,0:T(8,128)S(1)}, u32[]{:S(2)}, u32[]{:S(2)}) collective-permute-start(f32[96,1024]{1,0:T(8,128)S(1)} %collective-permute-done.refs_1_), channel_id=1, source_target_pairs={{0,32},{32,64},{64,96},{96,128},{128,160},{160,192},{192,224},{224... | collective-permute-start | bytes 1179656 | tf_op jit(solution)/shard_map/ppermute | solution.py:18
  44.6 43.2 %copy-start.4 = (f32[96,1024]{1,0:T(8,128)}, f32[96,1024]{1,0:T(8,128)S(1)}, u32[]{:S(2)}) copy-start(f32[96,1024]{1,0:T(8,128)S(1)} %collective-permute-done.3.refs_4_) | copy-start | bytes 1179652
  44.6 12.5 %collective-permute-start.5 = (f32[96,1024]{1,0:T(8,128)S(1)}, f32[96,1024]{1,0:T(8,128)S(1)}, u32[]{:S(2)}, u32[]{:S(2)}) collective-permute-start(f32[96,1024]{1,0:T(8,128)S(1)} %collective-permute-done.3.refs_4_), channel_id=1, source_target_pairs={{0,480},{32,0},{64,32},{96,64},{128,96},{160,128},{192,160},{224,1... | collective-permute-start | bytes 1179656 | tf_op jit(solution)/shard_map/ppermute | solution.py:18
  50.2 12.5 %collective-permute-start.4 = (f32[96,1024]{1,0:T(8,128)S(1)}, f32[96,1024]{1,0:T(8,128)S(1)}, u32[]{:S(2)}, u32[]{:S(2)}) collective-permute-start(f32[96,1024]{1,0:T(8,128)S(1)} %collective-permute-done.2.refs_3_), channel_id=1, source_target_pairs={{0,32},{32,64},{64,96},{96,128},{128,160},{160,192},{192,224},{224... | collective-permute-start | bytes 1179656 | tf_op jit(solution)/shard_map/ppermute | solution.py:18
  57.1 41.8 %copy-start.6 = (f32[96,1024]{1,0:T(8,128)}, f32[96,1024]{1,0:T(8,128)S(1)}, u32[]{:S(2)}) copy-start(f32[96,1024]{1,0:T(8,128)S(1)} %collective-permute-done.5.refs_6_) | copy-start | bytes 1179652
  57.1 11.7 %collective-permute-start.7 = (f32[96,1024]{1,0:T(8,128)S(1)}, f32[96,1024]{1,0:T(8,128)S(1)}, u32[]{:S(2)}, u32[]{:S(2)}) collective-permute-start(f32[96,1024]{1,0:T(8,128)S(1)} %collective-permute-done.5.refs_6_), channel_id=1, source_target_pairs={{0,480},{32,0},{64,32},{96,64},{128,96},{160,128},{192,160},{224,1... | collective-permute-start | bytes 1179656 | tf_op jit(solution)/shard_map/ppermute | solution.py:18
  62.8 11.6 %collective-permute-start.6 = (f32[96,1024]{1,0:T(8,128)S(1)}, f32[96,1024]{1,0:T(8,128)S(1)}, u32[]{:S(2)}, u32[]{:S(2)}) collective-permute-start(f32[96,1024]{1,0:T(8,128)S(1)} %collective-permute-done.4.refs_5_), channel_id=1, source_target_pairs={{0,32},{32,64},{64,96},{96,128},{128,160},{160,192},{192,224},{224... | collective-permute-start | bytes 1179656 | tf_op jit(solution)/shard_map/ppermute | solution.py:18
  68.8 10.9 %collective-permute-start.9 = (f32[96,1024]{1,0:T(8,128)S(1)}, f32[96,1024]{1,0:T(8,128)S(1)}, u32[]{:S(2)}, u32[]{:S(2)}) collective-permute-start(f32[96,1024]{1,0:T(8,128)S(1)} %collective-permute-done.7.refs_8_), channel_id=1, source_target_pairs={{0,480},{32,0},{64,32},{96,64},{128,96},{160,128},{192,160},{224,1... | collective-permute-start | bytes 1179656 | tf_op jit(solution)/shard_map/ppermute | solution.py:18
  74.4 10.9 %collective-permute-start.8 = (f32[96,1024]{1,0:T(8,128)S(1)}, f32[96,1024]{1,0:T(8,128)S(1)}, u32[]{:S(2)}, u32[]{:S(2)}) collective-permute-start(f32[96,1024]{1,0:T(8,128)S(1)} %collective-permute-done.6.refs_7_), channel_id=1, source_target_pairs={{0,32},{32,64},{64,96},{96,128},{128,160},{160,192},{192,224},{224... | collective-permute-start | bytes 1179656 | tf_op jit(solution)/shard_map/ppermute | solution.py:18
  79.7 10.9 %collective-permute-start.11 = (f32[96,1024]{1,0:T(8,128)S(1)}, f32[96,1024]{1,0:T(8,128)S(1)}, u32[]{:S(2)}, u32[]{:S(2)}) collective-permute-start(f32[96,1024]{1,0:T(8,128)S(1)} %collective-permute-done.9.refs_10_), channel_id=1, source_target_pairs={{0,480},{32,0},{64,32},{96,64},{128,96},{160,128},{192,160},{224,1... | collective-permute-start | bytes 1179656 | tf_op jit(solution)/shard_map/ppermute | solution.py:18
  85.3 11.1 %collective-permute-start.10 = (f32[96,1024]{1,0:T(8,128)S(1)}, f32[96,1024]{1,0:T(8,128)S(1)}, u32[]{:S(2)}, u32[]{:S(2)}) collective-permute-start(f32[96,1024]{1,0:T(8,128)S(1)} %collective-permute-done.8.refs_9_), channel_id=1, source_target_pairs={{0,32},{32,64},{64,96},{96,128},{128,160},{160,192},{192,224},{224... | collective-permute-start | bytes 1179656 | tf_op jit(solution)/shard_map/ppermute | solution.py:18
  90.5 11.9 %collective-permute-start.13 = (f32[96,1024]{1,0:T(8,128)S(1)}, f32[96,1024]{1,0:T(8,128)S(1)}, u32[]{:S(2)}, u32[]{:S(2)}) collective-permute-start(f32[96,1024]{1,0:T(8,128)S(1)} %collective-permute-done.11.refs_12_), channel_id=1, source_target_pairs={{0,480},{32,0},{64,32},{96,64},{128,96},{160,128},{192,160},{224,1... | collective-permute-start | bytes 1179656 | tf_op jit(solution)/shard_map/ppermute | solution.py:18
  96.4 12.2 %collective-permute-start.12 = (f32[96,1024]{1,0:T(8,128)S(1)}, f32[96,1024]{1,0:T(8,128)S(1)}, u32[]{:S(2)}, u32[]{:S(2)}) collective-permute-start(f32[96,1024]{1,0:T(8,128)S(1)} %collective-permute-done.10.refs_11_), channel_id=1, source_target_pairs={{0,32},{32,64},{64,96},{96,128},{128,160},{160,192},{192,224},{224... | collective-permute-start | bytes 1179656 | tf_op jit(solution)/shard_map/ppermute | solution.py:18
  102.5 15.5 %collective-permute-start.15 = (f32[48,1024]{1,0:T(8,128)S(1)}, f32[48,1024]{1,0:T(8,128)S(1)}, u32[]{:S(2)}, u32[]{:S(2)}) collective-permute-start(f32[48,1024]{1,0:T(8,128)S(1)} %slice.18), channel_id=1, source_target_pairs={{0,480},{32,0},{64,32},{96,64},{128,96},{160,128},{192,160},{224,1... | collective-permute-start | bytes 589832 | tf_op jit(solution)/shard_map/ppermute | solution.py:18
  108.6 8.8 %collective-permute-start.14 = (f32[48,1024]{1,0:T(8,128)S(1)}, f32[48,1024]{1,0:T(8,128)S(1)}, u32[]{:S(2)}, u32[]{:S(2)}) collective-permute-start(f32[48,1024]{1,0:T(8,128)S(1)} %slice.17), channel_id=1, source_target_pairs={{0,32},{32,64},{64,96},{96,128},{128,160},{160,192},{192,224},{224... | collective-permute-start | bytes 589832 | tf_op jit(solution)/shard_map/ppermute | solution.py:18
  111.1 48.9 %copy-start.16 = (s32[17]{0:T(128)S(1)}, s32[17]{0:T(128)}, u32[]{:S(2)}) copy-start(s32[17]{0:T(128)} %constant.153.clone) | copy-start | bytes 208
  111.1 48.9 %copy-start.17 = (s32[17]{0:T(128)S(1)}, s32[17]{0:T(128)}, u32[]{:S(2)}) copy-start(s32[17]{0:T(128)} %constant.152.clone) | copy-start | bytes 208
  117.3 43.2 %copy-start.15 = (f32[48,1024]{1,0:T(8,128)}, f32[48,1024]{1,0:T(8,128)S(1)}, u32[]{:S(2)}) copy-start(f32[48,1024]{1,0:T(8,128)S(1)} %collective-permute-done.14.refs_15_) | copy-start | bytes 589828
  118.0 42.5 %copy-start.14 = (f32[48,1024]{1,0:T(8,128)}, f32[48,1024]{1,0:T(8,128)S(1)}, u32[]{:S(2)}) copy-start(f32[48,1024]{1,0:T(8,128)S(1)} %collective-permute-done.15.refs_16_) | copy-start | bytes 589828
  154.3 12.5 %all-to-all-start.3 = ((f32[8,96,128]{2,1,0:T(8,128)}), f32[8,96,128]{2,1,0:T(8,128)S(1)}, u32[]{:S(2)}, u32[]{:S(2)}) async-start(f32[8,96,128]{2,1,0:T(8,128)} %broadcast_in_dim.11), calls=%async_computation.3 | async-start | bytes 786432 | tf_op jit(solution)/shard_map/all_to_all | solution.py:172
  (12 other events, 355.1 us)
